TPU v7x, 256 devices: a whole 4x4x8 slice. The times are simulated.
256 devices in a mesh: depth: 32 (over y_lo, z, core), shot: 8 (over x, y_hi).
Axes of the slice: x: 4, y: 4 (y_hi: 2, y_lo: 2; y = y_hi * 2 + y_lo), z: 8, core: 2. Of those that a mesh axis runs over, the one named last changes fastest.
Arguments:
- down_state: bfloat16 [64, 16, 2, 256, 256], P('depth', 'shot'), may hold values from -6 to 6
- up_state: bfloat16 [64, 16, 2, 256, 256], P('depth', 'shot'), may hold values from -6 to 6
- source: bfloat16 [16, 2, 256, 256], P('shot'), may hold values from -6 to 6
- reflect: float32 [64, 256, 256], P('depth'), may hold values from -0.3 to 0.3
- screen_class: int32 [64, 256, 256], P('depth'), may hold values from 0 to 15
- screen_values: float32 [16], replicated, may hold values from -1 to 1
- freq_index: int32 [16], P('shot'), may hold values from 0 to 127
Outputs:
- down_out: bfloat16 [64, 16, 2, 256, 256], P('depth', 'shot')
- up_out: bfloat16 [64, 16, 2, 256, 256], P('depth', 'shot')
- gradient: float32 [64, 256, 256], P('depth', 'shot')
All inputs are finite; a program needn't handle non-finite values.
Results may differ from a plain program's by a relative error of at most 0.034.
Values may be sent and summed in bfloat16 or wider, within the bound.
A program may use at most 64 MiB of HBM per device.

v0:
```python
import math

import jax
import jax.numpy as jnp
from jax import lax
from jax.sharding import PartitionSpec as P

HOPS = 3
NCLASS = 16
NFREQ = 128


def passed_along(block, axis, distance):
    devices = range(lax.axis_size(axis))
    route = [(i - distance, i) for i in devices if i - distance in devices]
    return lax.ppermute(block, axis, route)


def dft_tables(length):
    counter = jnp.arange(length, dtype=jnp.int32)
    product = counter[:, None] * counter[None, :] % length
    angles = 2.0 * math.pi / length * product.astype(jnp.float32)
    return (jnp.cos(angles).astype(jnp.bfloat16), jnp.sin(angles).astype(jnp.bfloat16))


def wavenumbers(length):
    counter = jnp.arange(length, dtype=jnp.int32)
    wrapped = jnp.where(counter >= length // 2, counter - length, counter)
    return 2.0 * math.pi / length * wrapped.astype(jnp.float32)


def propagate(planes, phase_re, phase_im, tables):
    fwd_left, fwd_right, inv_left, inv_right = tables
    first = jnp.einsum(
        "cdjk,...dkl->...cjl", fwd_left, planes, preferred_element_type=jnp.float32
    ).astype(jnp.bfloat16)
    second = jnp.einsum("...djl,dclm->...cjm", first, fwd_right, preferred_element_type=jnp.float32)
    real_part = second[..., 0, :, :]
    imag_part = second[..., 1, :, :]
    turned = jnp.stack(
        [real_part * phase_re - imag_part * phase_im, real_part * phase_im + imag_part * phase_re],
        axis=-3,
    ).astype(jnp.bfloat16)
    third = jnp.einsum(
        "cdjk,...dkl->...cjl", inv_left, turned, preferred_element_type=jnp.float32
    ).astype(jnp.bfloat16)
    return jnp.einsum(
        "...djl,dclm->...cjm", third, inv_right, preferred_element_type=jnp.float32
    ).astype(jnp.bfloat16)


def trade(down_edge, up_edge):
    got_down = passed_along(down_edge, "depth", 1)
    got_up = passed_along(up_edge, "depth", -1)
    return (got_down, got_up)


def per_device(down_state, up_state, source, reflect, screen_class, screen_values, freq_index):
    levels = down_state.shape[0]
    rows_x = down_state.shape[3]
    rows_y = down_state.shape[4]
    front_count = down_state.shape[1]
    depth_rank = lax.axis_index("depth")
    scale = 1.0 / math.sqrt(front_count * lax.axis_size("shot"))
    cos_x, sin_x = dft_tables(rows_x)
    cos_y, sin_y = dft_tables(rows_y)
    tables = (
        jnp.stack([jnp.stack([cos_x, sin_x]), jnp.stack([-sin_x, cos_x])]),
        jnp.stack([jnp.stack([cos_y, -sin_y]), jnp.stack([sin_y, cos_y])]),
        jnp.stack([jnp.stack([cos_x, -sin_x]), jnp.stack([sin_x, cos_x])]),
        jnp.stack([jnp.stack([cos_y, sin_y]), jnp.stack([-sin_y, cos_y])]),
    )
    kwave = 0.95 * math.pi * (freq_index.astype(jnp.float32) + 1.0) / NFREQ
    kx_wave = wavenumbers(rows_x)
    ky_wave = wavenumbers(rows_y)
    vertical = kwave[:, None, None] ** 2 - kx_wave[None, :, None] ** 2 - ky_wave[None, None, :] ** 2
    propag = jnp.sqrt(jnp.maximum(vertical, 0.0))
    damping = jnp.exp(-jnp.sqrt(jnp.maximum(-vertical, 0.0))) / (rows_x * rows_y)
    phase_re = damping * jnp.cos(propag)
    phase_im = damping * jnp.sin(propag)
    classes = jnp.arange(NCLASS, dtype=jnp.int32)
    onehot = (screen_class[None] == classes[:, None, None, None]).astype(jnp.float32)
    slowness = jnp.einsum("c,clxy->lxy", screen_values, onehot, precision=lax.Precision.HIGHEST)
    angle = kwave[None, :, None, None] * slowness[:, None]
    screen_re = jnp.cos(angle)
    screen_im = jnp.sin(angle)
    refl = reflect[:, None]
    top_slab = depth_rank == 0
    down = down_state
    up = up_state
    a_re = a_im = b_re = b_im = None
    for repeat in range(HOPS):
        down_edge = down[levels - 1]
        up_edge = up[0]
        got_down, got_up = trade(down_edge, up_edge)
        got_down = jnp.where(top_slab, source, got_down)
        moved = propagate(
            jnp.concatenate([got_down[None], down[: levels - 1], up[1:], got_up[None]], axis=0),
            phase_re,
            phase_im,
            tables,
        )
        from_above = moved[:levels]
        from_below = moved[levels:]
        qa_re = from_above[:, :, 0].astype(jnp.float32)
        qa_im = from_above[:, :, 1].astype(jnp.float32)
        qb_re = from_below[:, :, 0].astype(jnp.float32)
        qb_im = from_below[:, :, 1].astype(jnp.float32)
        a_re = screen_re * qa_re - screen_im * qa_im
        a_im = screen_re * qa_im + screen_im * qa_re
        b_re = screen_re * qb_re - screen_im * qb_im
        b_im = screen_re * qb_im + screen_im * qb_re
        down = jnp.stack(
            [(1.0 + refl) * a_re - refl * b_re, (1.0 + refl) * a_im - refl * b_im], axis=2
        ).astype(jnp.bfloat16)
        up = jnp.stack(
            [(1.0 - refl) * b_re + refl * a_re, (1.0 - refl) * b_im + refl * a_im], axis=2
        ).astype(jnp.bfloat16)
    terms = scale * jnp.sum(a_re * b_re + a_im * b_im, axis=1)
    gradient = lax.psum_scatter(
        terms.astype(jnp.bfloat16), "shot", scatter_dimension=1, tiled=True
    ).astype(jnp.float32)
    return (down, up, gradient)


def solution(mesh):
    return jax.shard_map(
        per_device,
        mesh=mesh,
        in_specs=(
            P("depth", "shot", None, None, None),
            P("depth", "shot", None, None, None),
            P("shot", None, None, None),
            P("depth", None, None),
            P("depth", None, None),
            P(),
            P("shot"),
        ),
        out_specs=(
            P("depth", "shot", None, None, None),
            P("depth", "shot", None, None, None),
            P("depth", "shot", None),
        ),
        check_vma=False,
    )
```

profile of v0, /device:TPU:24, one launch (start us, length us, event | category | flops | bytes accessed | tf_op | source)
XLA Modules:
  0.0 260.3 jit_solution(6953302592640487767)
XLA Ops:
  7.2 2.1 fusion.204
  10.4 1.9 collective-permute-start
  14.2 7.4 %collective-permute-start.1 = (bf16[2,2,256,256]{2,3,1,0:T(8,128)(2,1)}, bf16[2,2,256,256]{2,3,1,0:T(8,128)(2,1)}, u32[]{:S(2)}, u32[]{:S(2)}) collective-permute-start(bf16[2,2,256,256]{2,3,1,0:T(8,128)(2,1)} %bitcast.18), channel_id=1, source_target_pairs={{8,0},{16,8},{24,16},{32,24},{40,32},{48,40},{56,48},{64,56},{72,6... | collective-permute-start | bytes 1572872 | tf_op jit(solution)/shard_map/ppermute | solution.py:16
  21.6 2.3 iota_compare_fusion
  24.8 4.6 %fusion = f32[1,2,256,256]{3,0,2,1:T(1,128)} fusion(pred[16,2,256,256]{3,2,1,0:T(32,128)(4,1)S(1)} %iota_compare_fusion, f32[16]{0:T(128)S(1)} %copy-done), kind=kOutput, calls=%fused_computation.1 | convolution fusion | flops 25165824 | bytes 2621504 | tf_op jit(solution)/shard_map/c,clxy->lxy/dot_general | solution.py:83
  34.9 2.0 copy.248
  37.9 2.3 fusion.160
  42.1 6.1 %convolution_bitcast_fusion.2 = f32[4,2,2,256,256]{3,4,1,0,2:T(8,128)} fusion(bf16[1,2,2,256,256]{3,4,2,1,0:T(8,128)(2,1)} %bitcast.19, bf16[1,2,2,256,256]{3,4,2,1,0:T(8,128)(2,1)} %copy.248, bf16[1,2,2,256,256]{3,4,2,1,0:T(8,128)(2,1)} %copy.247, bf16[1,2,2,256,256]{3,4,2,1,0:T(8,128)(2,1)} %select_bitcast_fusion.2, ...), kind=kOutput, calls=%fused_computation.33 | convolution fusion | flops 2158231552 | bytes 7340032 | tf_op jit(solution)/shard_map/...djl,dclm->...cjm/dot_general | solution.py:37
  48.2 4.2 %subtract_convert_fusion.2 = (bf16[4,2,1,256,256]{3,4,1,0,2:T(8,128)(2,1)}, bf16[4,2,1,256,256]{3,4,1,0,2:T(8,128)(2,1)}) fusion(f32[4,2,2,256,256]{3,4,1,0,2:T(8,128)} %convolution_bitcast_fusion.2, f32[2,256,256]{1,2,0:T(8,128)S(1)} %get-tuple-element.46, f32[2,256,256]{1,2,0:T(8,128)S(1)} %get-tuple-element.45), kind=kLoop, calls=%fused_computation.76 | loop fusion | flops 4194304 | bytes 7340032 | tf_op jit(solution)/shard_map/convert.20
  52.4 5.5 %fusion.43 = bf16[4,2,2,256,256]{3,4,1,2,0:T(8,128)(2,1)} fusion(bf16[1,2,256,256]{3,2,1,0:T(8,128)(2,1)} %get-tuple-element.40, bf16[1,2,256,256]{3,2,1,0:T(8,128)(2,1)} %get-tuple-element.43, bf16[4,2,1,256,256]{3,4,1,0,2:T(8,128)(2,1)} %get-tuple-element.17, bf16[4,2,1,256,256]{3,4,1,0,2:T(8,128)(2,1)} %get-tuple-element.16, ...), kind=kOutput, calls=%fused_computation.77 | convolution fusion | flops 2151940096 | bytes 5242880 | tf_op jit(solution)/shard_map/...djl,dclm->...cjm/dot_general | solution.py:47
  57.9 7.4 %fusion.111 = (bf16[2,2,1,256,256]{3,4,1,2,0:T(8,128)(2,1)S(1)}, bf16[2,2,1,256,256]{3,4,1,2,0:T(8,128)(2,1)S(1)}, bf16[2,2,1,256,256]{3,4,1,0,2:T(8,128)(2,1)S(1)}) fusion(f32[2,256,256]{1,2,0:T(8,128)S(1)} %copy.120, f32[2,256,256]{1,2,0:T(8,128)S(1)} %bitcast.584, f32[2]{0:T(128)S(1)} %get-tuple-element.48, f32[2,256,256]{1,2,0:T(8,128)S(1)} %copy.105, ...), kind=kLoop, calls=%fused_computation.160 | loop fusion | flops 7602176 | bytes 5767176 | tf_op jit(solution)/shard_map/convert.18
  66.2 1.9 collective-permute-start.2
  68.2 4.5 %fusion.122 = bf16[2,2,1,256,256]{3,4,1,0,2:T(8,128)(2,1)S(1)} fusion(f32[2,256,256]{1,2,0:T(8,128)S(1)} %copy.134, f32[2,256,256]{1,2,0:T(8,128)S(1)} %copy.120, f32[2,256,256]{1,2,0:T(8,128)S(1)} %bitcast.585, f32[2]{0:T(128)S(1)} %get-tuple-element.48, bf16[4,2,2,256,256]{3,4,1,2,0:T(8,128)(2,1)S(1)} %copy-done.5), kind=kLoop, calls=%fused_computation.171 | loop fusion | flops 3932160 | bytes 4194312 | tf_op jit(solution)/shard_map/convert.17
  73.8 6.0 %collective-permute-start.3 = (bf16[2,2,256,256]{2,3,0,1:T(8,128)(2,1)}, bf16[2,2,256,256]{2,3,0,1:T(8,128)(2,1)}, u32[]{:S(2)}, u32[]{:S(2)}) collective-permute-start(bf16[2,2,256,256]{2,3,0,1:T(8,128)(2,1)} %get-tuple-element.32), channel_id=1, source_target_pairs={{8,0},{16,8},{24,16},{32,24},{40,32},{48,40},{56,48},{64,56},{72,6... | collective-permute-start | bytes 1572872 | tf_op jit(solution)/shard_map/ppermute | solution.py:16
  79.8 2.0 copy.133
  83.7 2.8 %collective-permute-done.3 = bf16[2,2,256,256]{2,3,0,1:T(8,128)(2,1)} collective-permute-done((bf16[2,2,256,256]{2,3,0,1:T(8,128)(2,1)}, bf16[2,2,256,256]{2,3,0,1:T(8,128)(2,1)}, u32[]{:S(2)}, u32[]{:S(2)}) %collective-permute-start.3) | collective-permute-done | bytes 524320 | tf_op jit(solution)/shard_map/ppermute | solution.py:16
  86.6 6.3 %convolution_bitcast_fusion.1 = f32[4,2,2,256,256]{3,4,1,0,2:T(8,128)} fusion(bf16[1,2,256,256]{3,2,1,0:T(8,128)(2,1)} %get-tuple-element.44, bf16[1,2,256,256]{3,2,1,0:T(8,128)(2,1)S(1)} %get-tuple-element.39, bf16[2,2,1,256,256]{3,4,1,2,0:T(8,128)(2,1)} %copy-done.11, bf16[2,2,1,256,256]{3,4,1,2,0:T(8,128)(2,1)} %copy-done.10, ...), kind=kOutput, calls=%fused_computation.32 | convolution fusion | flops 2165571584 | bytes 7864320 | tf_op jit(solution)/shard_map/...djl,dclm->...cjm/dot_general | solution.py:37
  92.8 4.2 %subtract_convert_fusion.1 = (bf16[4,2,1,256,256]{3,4,1,0,2:T(8,128)(2,1)}, bf16[4,2,1,256,256]{3,4,1,0,2:T(8,128)(2,1)}) fusion(f32[4,2,2,256,256]{3,4,1,0,2:T(8,128)} %convolution_bitcast_fusion.1, f32[2,256,256]{1,2,0:T(8,128)S(1)} %get-tuple-element.46, f32[2,256,256]{1,2,0:T(8,128)S(1)} %get-tuple-element.45), kind=kLoop, calls=%fused_computation.74 | loop fusion | flops 4194304 | bytes 7340032 | tf_op jit(solution)/shard_map/convert.14
  97.0 5.5 %fusion.46 = bf16[4,2,2,256,256]{3,4,1,0,2:T(8,128)(2,1)} fusion(bf16[1,2,256,256]{3,2,1,0:T(8,128)(2,1)} %get-tuple-element.40, bf16[1,2,256,256]{3,2,1,0:T(8,128)(2,1)} %get-tuple-element.43, bf16[4,2,1,256,256]{3,4,1,0,2:T(8,128)(2,1)} %get-tuple-element.15, bf16[4,2,1,256,256]{3,4,1,0,2:T(8,128)(2,1)} %get-tuple-element.14, ...), kind=kOutput, calls=%fused_computation.78 | convolution fusion | flops 2151940096 | bytes 5242880 | tf_op jit(solution)/shard_map/...djl,dclm->...cjm/dot_general | solution.py:47
  102.5 7.3 %fusion.124 = (bf16[2,2,1,256,256]{3,4,2,1,0:T(8,128)(2,1)S(1)}, bf16[2,2,1,256,256]{3,4,2,1,0:T(8,128)(2,1)S(1)}) fusion(f32[2,256,256]{1,2,0:T(8,128)S(1)} %copy.120, f32[2,256,256]{1,2,0:T(8,128)S(1)} %bitcast.586, f32[2]{0:T(128)S(1)} %get-tuple-element.48, f32[2,256,256]{1,2,0:T(8,128)S(1)} %copy.105, bf16[4,2,2,256,256]{3,4,1,0,2:T(8,128)(2,1)} %fusion.46), kind=kLoop, calls=%fused_computation.173 | loop fusion | flops 6553600 | bytes 4718600 | tf_op jit(solution)/shard_map/convert.12
  110.8 1.9 collective-permute-start.4
  112.8 4.9 %fusion.115 = (bf16[2,2,1,256,256]{3,4,2,1,0:T(8,128)(2,1)S(1)}, bf16[2,2,1,256,256]{3,4,2,1,0:T(8,128)(2,1)S(1)}) fusion(f32[2,256,256]{1,2,0:T(8,128)S(1)} %copy.134, f32[2,256,256]{1,2,0:T(8,128)S(1)} %copy.120, f32[2,256,256]{1,2,0:T(8,128)S(1)} %bitcast.587, f32[2]{0:T(128)S(1)} %get-tuple-element.48, bf16[4,2,2,256,256]{3,4,1,0,2:T(8,128)(2,1)S(1)} %copy-done.4), kind=kLoop, calls=%fused_computation.164 | loop fusion | flops 6553600 | bytes 4718600 | tf_op jit(solution)/shard_map/convert.10
  118.8 6.2 %collective-permute-start.5 = (bf16[2,2,256,256]{2,3,1,0:T(8,128)(2,1)}, bf16[2,2,256,256]{2,3,1,0:T(8,128)(2,1)}, u32[]{:S(2)}, u32[]{:S(2)}) collective-permute-start(bf16[2,2,256,256]{2,3,1,0:T(8,128)(2,1)} %get-tuple-element.30), channel_id=1, source_target_pairs={{8,0},{16,8},{24,16},{32,24},{40,32},{48,40},{56,48},{64,56},{72,6... | collective-permute-start | bytes 1572872 | tf_op jit(solution)/shard_map/ppermute | solution.py:16
  126.3 1.9 select_bitcast_fusion
  128.2 3.6 %collective-permute-done.5 = bf16[2,2,256,256]{2,3,1,0:T(8,128)(2,1)} collective-permute-done((bf16[2,2,256,256]{2,3,1,0:T(8,128)(2,1)}, bf16[2,2,256,256]{2,3,1,0:T(8,128)(2,1)}, u32[]{:S(2)}, u32[]{:S(2)}) %collective-permute-start.5) | collective-permute-done | bytes 524320 | tf_op jit(solution)/shard_map/ppermute | solution.py:16
  131.8 6.1 %convolution_bitcast_fusion = f32[4,2,2,256,256]{3,4,1,0,2:T(8,128)} fusion(bf16[2,2,1,256,256]{3,4,2,1,0:T(8,128)(2,1)} %copy-done.9, bf16[2,2,1,256,256]{3,4,2,1,0:T(8,128)(2,1)S(1)} %copy-done.8, bf16[1,2,2,256,256]{3,4,2,1,0:T(8,128)(2,1)} %bitcast.94, bf16[1,2,2,256,256]{3,4,2,1,0:T(8,128)(2,1)} %get-tuple-element.29, ...), kind=kOutput, calls=%fused_computation.31 | convolution fusion | flops 2165571584 | bytes 7864320 | tf_op jit(solution)/shard_map/...djl,dclm->...cjm/dot_general | solution.py:37
  137.9 4.2 %subtract_convert_fusion = (bf16[4,2,1,256,256]{3,4,1,0,2:T(8,128)(2,1)}, bf16[4,2,1,256,256]{3,4,1,0,2:T(8,128)(2,1)}) fusion(f32[4,2,2,256,256]{3,4,1,0,2:T(8,128)} %convolution_bitcast_fusion, f32[2,256,256]{1,2,0:T(8,128)S(1)} %get-tuple-element.46, f32[2,256,256]{1,2,0:T(8,128)S(1)} %get-tuple-element.45), kind=kLoop, calls=%fused_computation.72 | loop fusion | flops 4194304 | bytes 7340032 | tf_op jit(solution)/shard_map/convert.8
  142.1 4.1 %fusion.49 = bf16[4,2,2,256,256]{3,4,1,0,2:T(8,128)(2,1)S(1)} fusion(bf16[1,2,256,256]{3,2,1,0:T(8,128)(2,1)} %get-tuple-element.40, bf16[1,2,256,256]{3,2,1,0:T(8,128)(2,1)} %get-tuple-element.43, bf16[4,2,1,256,256]{3,4,1,0,2:T(8,128)(2,1)} %get-tuple-element.13, bf16[4,2,1,256,256]{3,4,1,0,2:T(8,128)(2,1)} %get-tuple-element.12, ...), kind=kOutput, calls=%fused_computation.79 | convolution fusion | flops 2151940096 | bytes 5242880 | tf_op jit(solution)/shard_map/...djl,dclm->...cjm/dot_general | solution.py:47
  146.2 7.5 %fusion.117 = (bf16[2,2,1,256,256]{3,4,2,1,0:T(8,128)(2,1)}, bf16[2,2,1,256,256]{3,4,2,1,0:T(8,128)(2,1)}) fusion(f32[2,256,256]{1,2,0:T(8,128)} %copy-done.1, f32[2,256,256]{1,2,0:T(8,128)S(1)} %copy.120, f32[2,256,256]{1,2,0:T(8,128)S(1)} %bitcast.588, f32[2]{0:T(128)S(1)} %get-tuple-element.48, bf16[4,2,2,256,256]{3,4,1,0,2:T(8,128)(2,1)S(1)} %fusion.49), kind=kLoop, calls=%fused_computation.166 | loop fusion | flops 6553600 | bytes 4718600 | tf_op jit(solution)/shard_map/convert.4
  153.7 4.9 %fusion.99 = f32[2,256,256]{1,2,0:T(8,128)S(1)} fusion(f32[2,256,256]{1,2,0:T(8,128)S(1)} %bitcast.589, f32[2]{0:T(128)S(1)} %get-tuple-element.48, bf16[4,2,2,256,256]{3,4,1,0,2:T(8,128)(2,1)S(1)} %fusion.49), kind=kLoop, calls=%fused_computation.148 | loop fusion | flops 5373952 | bytes 3145736 | tf_op jit(solution)/shard_map/reduce_sum | solution.py:119
  158.6 6.0 %fusion.128 = (bf16[2,2,1,256,256]{3,4,2,1,0:T(8,128)(2,1)}, bf16[2,2,1,256,256]{3,4,2,1,0:T(8,128)(2,1)}) fusion(f32[2,256,256]{1,2,0:T(8,128)S(1)} %copy.120, f32[2,256,256]{1,2,0:T(8,128)S(1)} %bitcast.590, f32[2]{0:T(128)S(1)} %get-tuple-element.48, f32[2,256,256]{1,2,0:T(8,128)S(1)} %copy-done.3, bf16[4,2,2,256,256]{3,4,1,0,2:T(8,128)(2,1)S(1)} %fusion.49), kind=kLoop, calls=%fused_computation.177 | loop fusion | flops 6553600 | bytes 4718600 | tf_op jit(solution)/shard_map/convert.6
  169.7 82.4 %all-reduce.3.cloned.1.call-done = bf16[2,256,256]{2,0,1:T(2,128)(2,1)} async-done(((bf16[2,256,256]{2,0,1:T(2,128)(2,1)}), bf16[2,256,256]{2,0,1:T(2,128)(2,1)}) %all-reduce.3.cloned.1.call-update) | async-done | bytes 262160
  (81 shorter events, 25.1 us)
Async XLA Ops:
  7.2 17.7 %copy-start = (f32[16]{0:T(128)S(1)}, f32[16]{0:T(128)}, u32[]{:S(2)}) copy-start(f32[16]{0:T(128)} %param.12) | copy-start | bytes 196
  7.2 5.1 %copy-start.18 = (bf16[2,2,2,256,256]{4,3,2,1,0:T(8,128)(2,1)S(1)}, bf16[2,2,2,256,256]{4,3,2,1,0:T(8,128)(2,1)}, u32[]{:S(2)}) copy-start(bf16[2,2,2,256,256]{4,3,2,1,0:T(8,128)(2,1)} %param.8) | copy-start | bytes 3145732
  7.2 244.9 %all-reduce.3.cloned.1.call-start = ((), (), s32[]{:S(2)}) async-start(), calls=%async_computation | async-start | bytes 524288
  9.4 12.2 %copy-start.20 = (s32[2]{0:T(128)S(1)}, s32[2]{0:T(128)}, u32[]{:S(2)}) copy-start(s32[2]{0:T(128)} %param.13) | copy-start | bytes 28
  10.4 29.8 %collective-permute-start = (bf16[2,2,256,256]{2,3,1,0:T(8,128)(2,1)}, bf16[2,2,256,256]{2,3,1,0:T(8,128)(2,1)}, u32[]{:S(2)}, u32[]{:S(2)}) collective-permute-start(bf16[2,2,256,256]{2,3,1,0:T(8,128)(2,1)} %bitcast.16), channel_id=1, source_target_pairs={{0,8},{8,16},{16,24},{24,32},{32,40},{40,48},{48,56},{56,64},{64,7... | collective-permute-start | bytes 1572872 | tf_op jit(solution)/shard_map/ppermute | solution.py:16
  13.2 10.7 %copy-start.12 = (f32[2,256,256]{2,1,0:T(8,128)S(1)}, f32[2,256,256]{2,1,0:T(8,128)}, u32[]{:S(2)}) copy-start(f32[2,256,256]{2,1,0:T(8,128)} %param.10) | copy-start | bytes 1572868
  14.2 27.9 %collective-permute-start.1 = (bf16[2,2,256,256]{2,3,1,0:T(8,128)(2,1)}, bf16[2,2,256,256]{2,3,1,0:T(8,128)(2,1)}, u32[]{:S(2)}, u32[]{:S(2)}) collective-permute-start(bf16[2,2,256,256]{2,3,1,0:T(8,128)(2,1)} %bitcast.18), channel_id=1, source_target_pairs={{8,0},{16,8},{24,16},{32,24},{40,32},{48,40},{56,48},{64,56},{72,6... | collective-permute-start | bytes 1572872 | tf_op jit(solution)/shard_map/ppermute | solution.py:16
  29.5 3.4 %copy-start.14 = (bf16[2,2,256,256]{3,2,1,0:T(8,128)(2,1)S(1)}, bf16[2,2,256,256]{3,2,1,0:T(8,128)(2,1)}, u32[]{:S(2)}) copy-start(bf16[2,2,256,256]{3,2,1,0:T(8,128)(2,1)} %param.9) | copy-start | bytes 1572868
  29.5 4.4 %copy-start.17 = (bf16[1,2,2,256,256]{4,3,2,1,0:T(8,128)(2,1)S(1)}, bf16[1,2,2,256,256]{4,3,2,1,0:T(8,128)(2,1)}, u32[]{:S(2)}) copy-start(bf16[1,2,2,256,256]{4,3,2,1,0:T(8,128)(2,1)} %get-tuple-element.34) | copy-start | bytes 1572868
  32.8 4.1 %copy-start.19 = (f32[1,2,256,256]{3,0,2,1:T(1,128)S(1)}, f32[1,2,256,256]{3,0,2,1:T(1,128)}, u32[]{:S(2)}) copy-start(f32[1,2,256,256]{3,0,2,1:T(1,128)} %fusion) | copy-start | bytes 1572868
  33.9 3.8 %copy-start.13 = (f32[2,256,256]{2,1,0:T(8,128)S(1)}, f32[2,256,256]{2,1,0:T(8,128)}, u32[]{:S(2)}) copy-start(f32[2,256,256]{2,1,0:T(8,128)} %get-tuple-element.38) | copy-start | bytes 1572868
  37.6 75.1 %copy-start.1 = (f32[2,256,256]{1,2,0:T(8,128)}, f32[2,256,256]{1,2,0:T(8,128)S(1)}, u32[]{:S(2)}) copy-start(f32[2,256,256]{1,2,0:T(8,128)S(1)} %copy.134) | copy-start | bytes 1572868
  37.9 64.7 %copy-start.2 = (f32[2,256,256]{1,2,0:T(8,128)}, f32[2,256,256]{1,2,0:T(8,128)S(1)}, u32[]{:S(2)}) copy-start(f32[2,256,256]{1,2,0:T(8,128)S(1)} %copy.105) | copy-start | bytes 1572868
  57.9 10.3 %copy-start.5 = (bf16[4,2,2,256,256]{3,4,1,2,0:T(8,128)(2,1)S(1)}, bf16[4,2,2,256,256]{3,4,1,2,0:T(8,128)(2,1)}, u32[]{:S(2)}) copy-start(bf16[4,2,2,256,256]{3,4,1,2,0:T(8,128)(2,1)} %fusion.43) | copy-start | bytes 6291460
  65.3 7.4 %copy-start.10 = (bf16[2,2,1,256,256]{3,4,1,2,0:T(8,128)(2,1)}, bf16[2,2,1,256,256]{3,4,1,2,0:T(8,128)(2,1)S(1)}, u32[]{:S(2)}) copy-start(bf16[2,2,1,256,256]{3,4,1,2,0:T(8,128)(2,1)S(1)} %get-tuple-element.26) | copy-start | bytes 1572868
  65.3 7.4 %copy-start.11 = (bf16[2,2,1,256,256]{3,4,1,2,0:T(8,128)(2,1)}, bf16[2,2,1,256,256]{3,4,1,2,0:T(8,128)(2,1)S(1)}, u32[]{:S(2)}) copy-start(bf16[2,2,1,256,256]{3,4,1,2,0:T(8,128)(2,1)S(1)} %get-tuple-element.27) | copy-start | bytes 1572868
  66.2 15.6 %collective-permute-start.2 = (bf16[2,2,256,256]{2,3,0,1:T(8,128)(2,1)}, bf16[2,2,256,256]{2,3,0,1:T(8,128)(2,1)}, u32[]{:S(2)}, u32[]{:S(2)}) collective-permute-start(bf16[2,2,256,256]{2,3,0,1:T(8,128)(2,1)} %fusion.170), channel_id=1, source_target_pairs={{0,8},{8,16},{16,24},{24,32},{32,40},{40,48},{48,56},{56,64},{64,7... | collective-permute-start | bytes 1572872 | tf_op jit(solution)/shard_map/ppermute | solution.py:16
  73.8 12.7 %collective-permute-start.3 = (bf16[2,2,256,256]{2,3,0,1:T(8,128)(2,1)}, bf16[2,2,256,256]{2,3,0,1:T(8,128)(2,1)}, u32[]{:S(2)}, u32[]{:S(2)}) collective-permute-start(bf16[2,2,256,256]{2,3,0,1:T(8,128)(2,1)} %get-tuple-element.32), channel_id=1, source_target_pairs={{8,0},{16,8},{24,16},{32,24},{40,32},{48,40},{56,48},{64,56},{72,6... | collective-permute-start | bytes 1572872 | tf_op jit(solution)/shard_map/ppermute | solution.py:16
  102.5 10.2 %copy-start.4 = (bf16[4,2,2,256,256]{3,4,1,0,2:T(8,128)(2,1)S(1)}, bf16[4,2,2,256,256]{3,4,1,0,2:T(8,128)(2,1)}, u32[]{:S(2)}) copy-start(bf16[4,2,2,256,256]{3,4,1,0,2:T(8,128)(2,1)} %fusion.46) | copy-start | bytes 6291460
  109.9 7.8 %copy-start.7 = (bf16[2,2,1,256,256]{3,4,2,1,0:T(8,128)(2,1)}, bf16[2,2,1,256,256]{3,4,2,1,0:T(8,128)(2,1)S(1)}, u32[]{:S(2)}) copy-start(bf16[2,2,1,256,256]{3,4,2,1,0:T(8,128)(2,1)S(1)} %get-tuple-element.24) | copy-start | bytes 1572868
  109.9 7.8 %copy-start.9 = (bf16[2,2,1,256,256]{3,4,2,1,0:T(8,128)(2,1)}, bf16[2,2,1,256,256]{3,4,2,1,0:T(8,128)(2,1)S(1)}, u32[]{:S(2)}) copy-start(bf16[2,2,1,256,256]{3,4,2,1,0:T(8,128)(2,1)S(1)} %get-tuple-element.25) | copy-start | bytes 1572868
  110.8 15.5 %collective-permute-start.4 = (bf16[2,2,256,256]{2,3,1,0:T(8,128)(2,1)}, bf16[2,2,256,256]{2,3,1,0:T(8,128)(2,1)}, u32[]{:S(2)}, u32[]{:S(2)}) collective-permute-start(bf16[2,2,256,256]{2,3,1,0:T(8,128)(2,1)} %fusion.166), channel_id=1, source_target_pairs={{0,8},{8,16},{16,24},{24,32},{32,40},{40,48},{48,56},{56,64},{64,7... | collective-permute-start | bytes 1572872 | tf_op jit(solution)/shard_map/ppermute | solution.py:16
  117.7 7.3 %copy-start.21 = (u32[256]{0:T(256)S(1)}, u32[256]{0:T(256)}, u32[]{:S(2)}) copy-start(u32[256]{0:T(256)} %constant.57) | copy-start | bytes 3076
  117.7 8.6 %copy-start.6 = (bf16[2,2,256,256]{2,3,1,0:T(8,128)(2,1)S(1)}, bf16[2,2,256,256]{2,3,1,0:T(8,128)(2,1)}, u32[]{:S(2)}) copy-start(bf16[2,2,256,256]{2,3,1,0:T(8,128)(2,1)} %copy.155) | copy-start | bytes 1572868
  117.7 14.0 %copy-start.8 = (bf16[2,2,1,256,256]{3,4,2,1,0:T(8,128)(2,1)S(1)}, bf16[2,2,1,256,256]{3,4,2,1,0:T(8,128)(2,1)}, u32[]{:S(2)}) copy-start(bf16[2,2,1,256,256]{3,4,2,1,0:T(8,128)(2,1)} %copy-done.7) | copy-start | bytes 1572868
  118.8 12.9 %collective-permute-start.5 = (bf16[2,2,256,256]{2,3,1,0:T(8,128)(2,1)}, bf16[2,2,256,256]{2,3,1,0:T(8,128)(2,1)}, u32[]{:S(2)}, u32[]{:S(2)}) collective-permute-start(bf16[2,2,256,256]{2,3,1,0:T(8,128)(2,1)} %get-tuple-element.30), channel_id=1, source_target_pairs={{8,0},{16,8},{24,16},{32,24},{40,32},{48,40},{56,48},{64,56},{72,6... | collective-permute-start | bytes 1572872 | tf_op jit(solution)/shard_map/ppermute | solution.py:16
  153.7 4.9 %copy-start.3 = (f32[2,256,256]{1,2,0:T(8,128)S(1)}, f32[2,256,256]{1,2,0:T(8,128)}, u32[]{:S(2)}) copy-start(f32[2,256,256]{1,2,0:T(8,128)} %copy-done.2) | copy-start | bytes 1572868
  165.6 2.7 %copy-start.15 = (bf16[2,2,1,256,256]{3,4,2,1,0:T(8,128)(2,1)S(1)}, bf16[2,2,1,256,256]{3,4,2,1,0:T(8,128)(2,1)}, u32[]{:S(2)}) copy-start(bf16[2,2,1,256,256]{3,4,2,1,0:T(8,128)(2,1)} %get-tuple-element.20) | copy-start | bytes 1572868
  165.6 2.7 %copy-start.16 = (bf16[2,2,1,256,256]{3,4,2,1,0:T(8,128)(2,1)S(1)}, bf16[2,2,1,256,256]{3,4,2,1,0:T(8,128)(2,1)}, u32[]{:S(2)}) copy-start(bf16[2,2,1,256,256]{3,4,2,1,0:T(8,128)(2,1)} %get-tuple-element.21) | copy-start | bytes 1572868
Sparse Core Ops, SparseCore 0:
  165.7 86.3 all-reduce.2
where the time goes:
time: 265 us; the launch traced here: 260 us
  waiting for transfers between devices  88.8 us (34%)
  other arithmetic  75.9 us (29%)
  matrix products  38.2 us (14%)
  starting transfers between devices  25.3 us (10%)
  local copies, waits for them, and re-layouts  17.1 us (6%)
  between operations  15.1 us (6%)
    unnamed x2, waiting for transfers between devices  82.4 us
    another operation x9, other arithmetic  50.3 us
    ppermute x6, starting transfers between devices, passed_along(): return lax.ppermute(block, axis, route)  25.2 us
    dot_general x3, matrix products, propagate(): jnp.einsum('...djl,dclm->...cjm', first, fwd_right, preferred_element_typ...  18.5 us
    dot_general x3, matrix products, propagate(): jnp.einsum('...djl,dclm->...cjm', third, inv_right, preferred_element_typ...  15.1 us
    unnamed x55, local copies, waits for them, and re-layouts  12.2 us
    ppermute x6, waiting for transfers between devices, passed_along(): return lax.ppermute(block, axis, route)  6.38 us
    broadcast_in_dim x3, other arithmetic, per_device(): got_down[None]  5.71 us
  transfers between devices with their start and end apart: 7, of which 3 were waited for; matrix products, arithmetic and copies ran while one was open for 17% of the time, Pallas kernels for 0%

commit v1 on v0

v1 whole, which is shorter than its diff:
```python
import math

import jax
import jax.numpy as jnp
import numpy as np
from jax import lax
from jax.experimental import pallas as pl
from jax.experimental.pallas import tpu as pltpu
from jax.sharding import PartitionSpec as P

HOPS = 3
NCLASS = 16
NFREQ = 128
N = 256
H = N // 2
MESH = pl.DeviceIdType.MESH
BF16 = jnp.bfloat16
F32 = jnp.float32
COS_COEFS = [(-1.0) ** k / math.factorial(2 * k) for k in range(10)]
SIN_COEFS = [(-1.0) ** k / math.factorial(2 * k + 1) for k in range(10)]


def half_tables():
    row = np.arange(H)[:, None]
    col = np.arange(H)[None, :]
    mats = []
    for parity in (0, 1):
        angle = (2.0 * math.pi / N) * (((2 * row + parity) * col) % N).astype(np.float64)
        cos, sin = np.cos(angle), np.sin(angle)
        fwd = np.block([[cos, sin], [-sin, cos]])
        mats.append(fwd)
        mats.append(fwd.T)
    return np.stack(mats).astype(np.float32)


def poly(coefs, q):
    acc = jnp.full_like(q, coefs[-1])
    for c in coefs[-2::-1]:
        acc = acc * q + c
    return acc


def dot(a, b):
    return jnp.dot(a, b, preferred_element_type=F32)


def kernel(
    groups,
    slabs,
    screen_values,
    freq_index,
    down_hbm,
    up_hbm,
    source_hbm,
    reflect_hbm,
    class_hbm,
    table_hbm,
    down_out,
    up_out,
    grad_out,
    tab,
    classes,
    refl,
    local,
    halo,
    edge,
    inner,
    phase,
    screen,
    lut,
    s2,
    s3,
    s4,
    gsum,
    gsend,
    grecv,
    load_sem,
    src_sem,
    send_sem,
    recv_sem,
    gsend_sem,
    grecv_sem,
):
    d = lax.axis_index("depth")
    s = lax.axis_index("shot")
    has_above = d > 0
    has_below = d < slabs - 1

    loads = [
        pltpu.make_async_copy(table_hbm, tab, load_sem.at[0]),
        pltpu.make_async_copy(class_hbm, classes, load_sem.at[1]),
        pltpu.make_async_copy(reflect_hbm, refl, load_sem.at[2]),
        pltpu.make_async_copy(down_hbm.at[0], local.at[0], load_sem.at[3]),
        pltpu.make_async_copy(up_hbm.at[1], local.at[1], load_sem.at[4]),
    ]
    for c in loads:
        c.start()

    barrier = pltpu.get_barrier_semaphore()

    @pl.when(has_above)
    def _():
        pl.semaphore_signal(barrier, inc=1, device_id={"depth": d - 1}, device_id_type=MESH)

    @pl.when(has_below)
    def _():
        pl.semaphore_signal(barrier, inc=1, device_id={"depth": d + 1}, device_id_type=MESH)

    for o in range(1, groups):
        pl.semaphore_signal(
            barrier, inc=1, device_id={"shot": lax.rem(s + o, groups)}, device_id_type=MESH
        )
    pl.semaphore_wait(
        barrier, groups - 1 + has_above.astype(jnp.int32) + has_below.astype(jnp.int32)
    )

    def to_below(src, h, f):
        return pltpu.make_async_remote_copy(
            src_ref=src,
            dst_ref=halo.at[h, 0, f],
            send_sem=send_sem.at[h, 0, f],
            recv_sem=recv_sem.at[h, 0, f],
            device_id={"depth": lax.rem(d + 1, slabs)},
            device_id_type=MESH,
        )

    def to_above(src, h, f):
        return pltpu.make_async_remote_copy(
            src_ref=src,
            dst_ref=halo.at[h, 1, f],
            send_sem=send_sem.at[h, 1, f],
            recv_sem=recv_sem.at[h, 1, f],
            device_id={"depth": lax.rem(d + slabs - 1, slabs)},
            device_id_type=MESH,
        )

    def from_source(h, f):
        return pltpu.make_async_copy(source_hbm.at[f], halo.at[h, 0, f], src_sem.at[h, f])

    for f in range(2):

        @pl.when(has_below)
        def _():
            to_below(down_hbm.at[1, f], 0, f).start()

        @pl.when(has_above)
        def _():
            to_above(up_hbm.at[0, f], 0, f).start()

    @pl.when(jnp.logical_not(has_above))
    def _():
        for h in range(HOPS):
            for f in range(2):
                from_source(h, f).start()

    @pl.when(jnp.logical_not(has_below))
    def _():
        def clear(t, carry):
            halo[t // 2, 1, lax.rem(t, 2)] = jnp.zeros((2, N, N), BF16)
            return carry

        lax.fori_loop(0, 2 * HOPS, clear, 0)

    kwave = [0.95 * math.pi * (freq_index[f].astype(F32) + 1.0) / NFREQ for f in range(2)]

    def fill_phase(t, carry):
        r0 = pl.multiple_of(t * 8, 8)
        row = lax.broadcasted_iota(jnp.int32, (8, N), 0) + r0
        lane = lax.broadcasted_iota(jnp.int32, (8, N), 1)
        ym = jnp.where(lane < H, 2 * lane, 2 * (lane - H) + 1)
        ym = jnp.where(ym >= H, ym - N, ym)
        ky = (2.0 * math.pi / N) * ym.astype(F32)
        for par in range(2):
            xm = 2 * row + par
            xm = jnp.where(xm >= H, xm - N, xm)
            kx = (2.0 * math.pi / N) * xm.astype(F32)
            k2 = kx * kx + ky * ky
            for f in range(2):
                q = kwave[f] * kwave[f] - k2
                root = jnp.sqrt(jnp.abs(q))
                qp = jnp.maximum(q, 0.0)
                damp = jnp.where(q < 0.0, jnp.exp(-root), 1.0) * (1.0 / (N * N))
                sin = jnp.where(q > 0.0, root, 0.0) * poly(SIN_COEFS, qp)
                phase[f, par, 0, pl.ds(r0, 8), :] = damp * poly(COS_COEFS, qp)
                phase[f, par, 1, pl.ds(r0, 8), :] = damp * sin
        return carry

    lax.fori_loop(0, H // 8, fill_phase, 0)

    for f in range(2):
        for c in range(NCLASS):
            ang = jnp.full((8, 128), kwave[f] * screen_values[c], F32)
            q = ang * ang
            lut[2 * f, c] = poly(COS_COEFS, q)
            lut[2 * f + 1, c] = ang * poly(SIN_COEFS, q)

    loads[1].wait()

    def fill_screen(t, carry):
        lev = t // (N // 8)
        r0 = pl.multiple_of(lax.rem(t, N // 8) * 8, 8)
        for half in range(2):
            cols = pl.ds(half * H, H)
            cls = classes[lev, pl.ds(r0, 8), cols]
            bits = [(cls & (1 << b)) != 0 for b in range(4)]
            for k in range(4):
                vals = [lut[k, c] for c in range(NCLASS)]
                for b in range(4):
                    vals = [
                        jnp.where(bits[b], vals[2 * i + 1], vals[2 * i])
                        for i in range(len(vals) // 2)
                    ]
                screen[lev, k // 2, k % 2, pl.ds(r0, 8), cols] = vals[0]
        return carry

    lax.fori_loop(0, 2 * N // 8, fill_screen, 0)
    loads[0].wait()
    loads[2].wait()
    loads[3].wait()
    loads[4].wait()

    def propagate(srcs, f):
        fe, ie, fo, io = 0, 1, 2, 3
        for i, src in enumerate(srcs):
            re_l, re_r = src[0, :, :H], src[0, :, H:]
            im_l, im_r = src[1, :, :H], src[1, :, H:]
            ev = dot(jnp.concatenate([re_l + re_r, im_l + im_r], axis=1), tab[ie])
            od = dot(jnp.concatenate([re_l - re_r, im_l - im_r], axis=1), tab[io])
            for j, x in enumerate((ev, od)):
                cols = slice(j * H, (j + 1) * H)
                u = (x[:H] + x[H:]).astype(BF16)
                v = (x[:H] - x[H:]).astype(BF16)
                s2[i, 0, :H, cols] = u[:, :H]
                s2[i, 0, H:, cols] = u[:, H:]
                s2[i, 1, :H, cols] = v[:, :H]
                s2[i, 1, H:, cols] = v[:, H:]
        for i in range(len(srcs)):
            for par, t in enumerate((fe, fo)):
                x = dot(tab[t], s2[i, par])
                pr, pi = phase[f, par, 0], phase[f, par, 1]
                re, im = x[:H], x[H:]
                s3[i, par, :H] = (re * pr - im * pi).astype(BF16)
                s3[i, par, H:] = (re * pi + im * pr).astype(BF16)
        for i in range(len(srcs)):
            e = dot(tab[ie], s3[i, 0])
            o = dot(tab[io], s3[i, 1])
            top = (e + o).astype(BF16)
            bot = (e - o).astype(BF16)
            for j in range(2):
                cols = slice(j * H, (j + 1) * H)
                s4[i, j, :H, :H] = top[:H, cols]
                s4[i, j, :H, H:] = top[H:, cols]
                s4[i, j, H:, :H] = bot[:H, cols]
                s4[i, j, H:, H:] = bot[H:, cols]
        outs = []
        for i in range(len(srcs)):
            e = dot(s4[i, 0], tab[fe])
            o = dot(s4[i, 1], tab[fo])
            outs.append((e + o, e - o))
        return outs

    def screened(x, lev, f, j):
        cols = slice(j * H, (j + 1) * H)
        sr, si = screen[lev, f, 0, :, cols], screen[lev, f, 1, :, cols]
        re, im = x[j][:, :H], x[j][:, H:]
        return (sr * re - si * im, sr * im + si * re)

    def inner_step(f):
        qa, qb = propagate((local.at[0, f], local.at[1, f]), f)
        for j in range(2):
            cols = slice(j * H, (j + 1) * H)
            for k, (x, lev) in enumerate(((qa, 1), (qb, 0))):
                re, im = screened(x, lev, f, j)
                inner[k, f, 0, :, cols] = re
                inner[k, f, 1, :, cols] = im

    def wait_halo(h, f):
        @pl.when(has_above)
        def _():
            to_below(halo.at[h, 0, f], h, f).wait_recv()

        @pl.when(jnp.logical_not(has_above))
        def _():
            from_source(h, f).wait()

        @pl.when(has_below)
        def _():
            to_above(halo.at[h, 1, f], h, f).wait_recv()

    def outer_step(h, f, dn1, up1, dn0, up0, grad):
        wait_halo(h, f)
        qa, qb = propagate((halo.at[h, 0, f], halo.at[h, 1, f]), f)
        for j in range(2):
            cols = slice(j * H, (j + 1) * H)
            a0 = screened(qa, 0, f, j)
            b1 = screened(qb, 1, f, j)
            r0, r1 = refl[0, :, cols], refl[1, :, cols]
            g0 = g1 = 0.0
            for c in range(2):
                b0 = inner[1, f, c, :, cols]
                a1 = inner[0, f, c, :, cols]
                t0 = r0 * (a0[c] - b0)
                t1 = r1 * (a1 - b1[c])
                dn1[c, :, cols] = (a1 + t1).astype(BF16)
                up0[c, :, cols] = (b0 + t0).astype(BF16)
                dn0[c, :, cols] = (a0[c] + t0).astype(BF16)
                up1[c, :, cols] = (b1[c] + t1).astype(BF16)
                g0 = g0 + a0[c] * b0
                g1 = g1 + a1 * b1[c]
            if grad is not None:
                grad(j, g0, g1)

    def first(f, carry):
        inner_step(f)
        return carry

    lax.fori_loop(0, 2, first, 0)

    def middle(t, carry):
        h, f = t // 2, lax.rem(t, 2)
        outer_step(
            h, f, edge.at[h, 0, f], local.at[1, f], local.at[0, f], edge.at[h, 1, f], None
        )

        @pl.when(has_below)
        def _():
            to_below(edge.at[h, 0, f], h + 1, f).start()

        @pl.when(has_above)
        def _():
            to_above(edge.at[h, 1, f], h + 1, f).start()

        inner_step(f)
        return carry

    lax.fori_loop(0, 2 * (HOPS - 1), middle, 0)

    scale = 1.0 / math.sqrt(2 * groups)

    def grad_first(j, g0, g1):
        cols = slice(j * H, (j + 1) * H)
        gsum[0, :, cols] = g0
        gsum[1, :, cols] = g1

    def grad_last(j, g0, g1):
        cols = slice(j * H, (j + 1) * H)
        rows = N // groups
        for lev, g in enumerate((g0, g1)):
            tot = ((gsum[lev, :, cols] + g) * scale).astype(BF16)
            for k in range(groups):
                gsend[k, lev, :, cols] = tot[k * rows : (k + 1) * rows]

    for f in range(2):
        outer_step(
            HOPS - 1,
            f,
            down_out.at[1, f],
            up_out.at[1, f],
            down_out.at[0, f],
            up_out.at[0, f],
            grad_last if f else grad_first,
        )

    def share(o):
        peer = lax.rem(s + o, groups)
        return pltpu.make_async_remote_copy(
            src_ref=gsend.at[peer],
            dst_ref=grecv.at[o - 1],
            send_sem=gsend_sem.at[o - 1],
            recv_sem=grecv_sem.at[o - 1],
            device_id={"shot": peer},
            device_id_type=MESH,
        )

    for o in range(1, groups):
        share(o).start()

    for h in range(HOPS):
        for f in range(2):

            @pl.when(has_below)
            def _():
                to_below(edge.at[0, 0, f], h, f).wait_send()

            @pl.when(has_above)
            def _():
                to_above(edge.at[0, 1, f], h, f).wait_send()

    total = gsend[s].astype(F32)
    for o in range(1, groups):
        share(o).wait_recv()
        total = total + grecv[o - 1].astype(F32)
    grad_out[...] = total
    for o in range(1, groups):
        share(o).wait_send()


def solution(mesh):
    groups = mesh.shape["shot"]
    slabs = mesh.shape["depth"]
    rows = N // groups

    def per_device(down_state, up_state, source, reflect, screen_class, screen_values, freq_index):
        table = jnp.asarray(half_tables(), BF16)
        hbm = pl.BlockSpec(memory_space=pl.ANY)
        smem = pl.BlockSpec(memory_space=pltpu.SMEM)
        vmem = pl.BlockSpec(memory_space=pltpu.VMEM)
        dma = pltpu.SemaphoreType.DMA
        return pl.pallas_call(
            lambda *refs: kernel(groups, slabs, *refs),
            out_shape=(
                jax.ShapeDtypeStruct(down_state.shape, BF16),
                jax.ShapeDtypeStruct(up_state.shape, BF16),
                jax.ShapeDtypeStruct((2, rows, N), F32),
            ),
            in_specs=[smem, smem, hbm, hbm, hbm, hbm, hbm, hbm],
            out_specs=(vmem, vmem, vmem),
            scratch_shapes=[
                pltpu.VMEM((4, N, N), BF16),
                pltpu.VMEM((2, N, N), jnp.int32),
                pltpu.VMEM((2, N, N), F32),
                pltpu.VMEM((2, 2, 2, N, N), BF16),
                pltpu.VMEM((HOPS, 2, 2, 2, N, N), BF16),
                pltpu.VMEM((HOPS - 1, 2, 2, 2, N, N), BF16),
                pltpu.VMEM((2, 2, 2, N, N), F32),
                pltpu.VMEM((2, 2, 2, H, N), F32),
                pltpu.VMEM((2, 2, 2, N, N), F32),
                pltpu.VMEM((4, NCLASS, 8, 128), F32),
                pltpu.VMEM((2, 2, N, N), BF16),
                pltpu.VMEM((2, 2, N, N), BF16),
                pltpu.VMEM((2, 2, N, N), BF16),
                pltpu.VMEM((2, N, N), F32),
                pltpu.VMEM((groups, 2, rows, N), BF16),
                pltpu.VMEM((groups - 1, 2, rows, N), BF16),
                dma((5,)),
                dma((HOPS, 2)),
                dma((HOPS, 2, 2)),
                dma((HOPS, 2, 2)),
                dma((groups - 1,)),
                dma((groups - 1,)),
            ],
            compiler_params=pltpu.CompilerParams(
                collective_id=0, has_side_effects=True, vmem_limit_bytes=56 * 1024 * 1024
            ),
        )(screen_values, freq_index, down_state, up_state, source, reflect, screen_class, table)

    return jax.shard_map(
        per_device,
        mesh=mesh,
        in_specs=(
            P("depth", "shot", None, None, None),
            P("depth", "shot", None, None, None),
            P("shot", None, None, None),
            P("depth", None, None),
            P("depth", None, None),
            P(),
            P("shot"),
        ),
        out_specs=(
            P("depth", "shot", None, None, None),
            P("depth", "shot", None, None, None),
            P("depth", "shot", None),
        ),
        check_vma=False,
    )
```

time: 265 us -> 47.9 us (0.18); the launches traced: 260 us -> 47.8 us
  waiting for transfers between devices: 88.8 us -> 0 us
  other arithmetic: 75.9 us -> 0 us
  Pallas kernels: 0 us -> 43.1 us
  matrix products: 38.2 us -> 0 us
  starting transfers between devices: 25.3 us -> 0 us
  between operations: 15.1 us -> 0.65 us
  local copies, waits for them, and re-layouts: 17.1 us -> 3.96 us
    unnamed x2 -> x0, waiting for transfers between devices: 82.4 us -> none
    another operation x13 -> x0, other arithmetic: 54 us -> none
    pallas_call x0 -> x1, Pallas kernels: none -> 43.1 us  [per_device(): pl.pallas_call(lambda *refs: kernel(groups, slabs, *refs), out_shape=(jax...]
    dot_general x7 -> x0, matrix products: 38.2 us -> none  [the longest x3 18.5 us: propagate(): jnp.einsum('...djl,dclm->...cjm', first, fwd_right, preferred_element_typ...]
    ppermute x6 -> x0, starting transfers between devices: 25.2 us -> none  [passed_along(): return lax.ppermute(block, axis, route)]
    unnamed x55 -> x7, local copies, waits for them, and re-layouts: 12.2 us -> 3.96 us
    ppermute x6 -> x0, waiting for transfers between devices: 6.38 us -> none  [passed_along(): return lax.ppermute(block, axis, route)]
    broadcast_in_dim x3 -> x0, other arithmetic: 5.71 us -> none  [per_device(): got_down[None]]
  transfers between devices with their start and end apart: 7 -> 0, of which waited for: 3 -> 0; matrix products, arithmetic and copies ran while one was open for 17% -> 0% of each run, Pallas kernels for 0% -> 0%
where the time goes in v1:
time: 47.9 us; the launch traced here: 47.8 us
  Pallas kernels  43.1 us (90%)
  local copies, waits for them, and re-layouts  3.96 us (8%)
  between operations  0.65 us (1%)
    pallas_call x1, Pallas kernels, per_device(): pl.pallas_call(lambda *refs: kernel(groups, slabs, *refs), out_shape=(jax...  43.1 us
    unnamed x7, local copies, waits for them, and re-layouts  3.96 us

profile of v1, /device:TPU:24, one launch (start us, length us, event | category | flops | bytes accessed | tf_op | source)
XLA Modules:
  0.0 47.8 jit_solution(3727025325178613863)
XLA Ops:
  0.6 43.1 %shard_map.103 = (bf16[2,2,2,256,256]{4,3,2,1,0:T(8,128)(2,1)}, bf16[2,2,2,256,256]{4,3,2,1,0:T(8,128)(2,1)}, f32[2,32,256]{2,1,0:T(8,128)}) custom-call(f32[16]{0:T(128)} %refs_0_.1, s32[2]{0:T(128)} %refs_1_.1, bf16[2,2,2,256,256]{4,3,2,1,0:T(8,128)(2,1)} %refs_2_.1, bf16[2,2,2,256,256]{4,3,2,1,0:T(8,128)(2,1)} %refs_3_.1, ...), custom_call_target="tpu_custom_call" | custom-call | tf_op jit(solution)/shard_map/pallas_call | solution.py:409
  43.8 0.0 copy-start
  43.8 2.4 %copy.14 = bf16[2,2,2,256,256]{4,3,2,1,0:T(8,128)(2,1)} copy(bf16[2,2,2,256,256]{4,3,2,1,0:T(8,128)(2,1)} %get-tuple-element.6) | data formatting | bytes 2097152
  46.1 0.0 copy-done
  46.1 0.0 copy-start.1
  46.2 1.0 %copy.15 = bf16[2,2,2,256,256]{4,3,2,1,0:T(8,128)(2,1)} copy(bf16[2,2,2,256,256]{4,3,2,1,0:T(8,128)(2,1)S(1)} %copy-done) | data formatting | bytes 2097152
  47.1 0.0 copy-done.1
  47.1 0.6 %copy.16 = f32[2,32,256]{2,1,0:T(8,128)} copy(f32[2,32,256]{2,1,0:T(8,128)S(1)} %copy-done.1) | data formatting | bytes 131072
Async XLA Ops:
  43.8 2.4 %copy-start = (bf16[2,2,2,256,256]{4,3,2,1,0:T(8,128)(2,1)S(1)}, bf16[2,2,2,256,256]{4,3,2,1,0:T(8,128)(2,1)}, u32[]{:S(2)}) copy-start(bf16[2,2,2,256,256]{4,3,2,1,0:T(8,128)(2,1)} %get-tuple-element.7) | copy-start | bytes 3145732
  46.1 1.0 %copy-start.1 = (f32[2,32,256]{2,1,0:T(8,128)S(1)}, f32[2,32,256]{2,1,0:T(8,128)}, u32[]{:S(2)}) copy-start(f32[2,32,256]{2,1,0:T(8,128)} %get-tuple-element.8) | copy-start | bytes 196612

commit v2 on v1

--- a/solution.py
+++ b/solution.py
@@ -47,8 +47,8 @@
 def kernel(
     groups,
     slabs,
-    screen_values,
-    freq_index,
+    values_hbm,
+    freq_hbm,
     down_hbm,
     up_hbm,
     source_hbm,
@@ -74,12 +74,15 @@
     gsum,
     gsend,
     grecv,
+    screen_values,
+    freq_index,
     load_sem,
     src_sem,
     send_sem,
     recv_sem,
     gsend_sem,
     grecv_sem,
+    near_sem,
 ):
     d = lax.axis_index("depth")
     s = lax.axis_index("shot")
@@ -92,9 +95,18 @@
         pltpu.make_async_copy(reflect_hbm, refl, load_sem.at[2]),
         pltpu.make_async_copy(down_hbm.at[0], local.at[0], load_sem.at[3]),
         pltpu.make_async_copy(up_hbm.at[1], local.at[1], load_sem.at[4]),
+        pltpu.make_async_copy(freq_hbm, freq_index, load_sem.at[5]),
+        pltpu.make_async_copy(values_hbm, screen_values, load_sem.at[6]),
     ]
-    for c in loads:
-        c.start()
+    near = [
+        lax.rem(s + 2, groups),
+        lax.rem(s + groups - 2, groups),
+        s + 1 - 2 * lax.rem(s, 2),
+    ]
+
+    def greet(sem):
+        for peer in near:
+            pl.semaphore_signal(sem, inc=1, device_id={"shot": peer}, device_id_type=MESH)
 
     barrier = pltpu.get_barrier_semaphore()
 
@@ -106,12 +118,11 @@
     def _():
         pl.semaphore_signal(barrier, inc=1, device_id={"depth": d + 1}, device_id_type=MESH)
 
-    for o in range(1, groups):
-        pl.semaphore_signal(
-            barrier, inc=1, device_id={"shot": lax.rem(s + o, groups)}, device_id_type=MESH
-        )
+    greet(barrier)
+    for c in loads[::-1]:
+        c.start()
     pl.semaphore_wait(
-        barrier, groups - 1 + has_above.astype(jnp.int32) + has_below.astype(jnp.int32)
+        barrier, len(near) + has_above.astype(jnp.int32) + has_below.astype(jnp.int32)
     )
 
     def to_below(src, h, f):
@@ -161,6 +172,8 @@
 
         lax.fori_loop(0, 2 * HOPS, clear, 0)
 
+    greet(near_sem.at[0])
+    loads[5].wait()
     kwave = [0.95 * math.pi * (freq_index[f].astype(F32) + 1.0) / NFREQ for f in range(2)]
 
     def fill_phase(t, carry):
@@ -187,6 +200,7 @@
 
     lax.fori_loop(0, H // 8, fill_phase, 0)
 
+    loads[6].wait()
     for f in range(2):
         for c in range(NCLASS):
             ang = jnp.full((8, 128), kwave[f] * screen_values[c], F32)
@@ -315,6 +329,8 @@
         return carry
 
     lax.fori_loop(0, 2, first, 0)
+    pl.semaphore_wait(near_sem.at[0], len(near))
+    greet(near_sem.at[1])
 
     def middle(t, carry):
         h, f = t // 2, lax.rem(t, 2)
@@ -372,6 +388,7 @@
             device_id_type=MESH,
         )
 
+    pl.semaphore_wait(near_sem.at[1], len(near))
     for o in range(1, groups):
         share(o).start()
 
@@ -395,6 +412,15 @@
         share(o).wait_send()
 
 
+def store(*refs):
+    sems = refs[-1]
+    copies = [pltpu.make_async_copy(refs[i], refs[i + 3], sems.at[i]) for i in range(3)]
+    for c in copies:
+        c.start()
+    for c in copies:
+        c.wait()
+
+
 def solution(mesh):
     groups = mesh.shape["shot"]
     slabs = mesh.shape["depth"]
@@ -402,18 +428,17 @@
 
     def per_device(down_state, up_state, source, reflect, screen_class, screen_values, freq_index):
         table = jnp.asarray(half_tables(), BF16)
-        hbm = pl.BlockSpec(memory_space=pl.ANY)
-        smem = pl.BlockSpec(memory_space=pltpu.SMEM)
+        hbm = pl.BlockSpec(memory_space=pltpu.HBM)
         vmem = pl.BlockSpec(memory_space=pltpu.VMEM)
         dma = pltpu.SemaphoreType.DMA
-        return pl.pallas_call(
+        results = pl.pallas_call(
             lambda *refs: kernel(groups, slabs, *refs),
             out_shape=(
-                jax.ShapeDtypeStruct(down_state.shape, BF16),
-                jax.ShapeDtypeStruct(up_state.shape, BF16),
-                jax.ShapeDtypeStruct((2, rows, N), F32),
+                pltpu.VMEM(down_state.shape, BF16),
+                pltpu.VMEM(up_state.shape, BF16),
+                pltpu.VMEM((2, rows, N), F32),
             ),
-            in_specs=[smem, smem, hbm, hbm, hbm, hbm, hbm, hbm],
+            in_specs=[hbm] * 8,
             out_specs=(vmem, vmem, vmem),
             scratch_shapes=[
                 pltpu.VMEM((4, N, N), BF16),
@@ -432,17 +457,41 @@
                 pltpu.VMEM((2, N, N), F32),
                 pltpu.VMEM((groups, 2, rows, N), BF16),
                 pltpu.VMEM((groups - 1, 2, rows, N), BF16),
-                dma((5,)),
+                pltpu.SMEM((NCLASS,), F32),
+                pltpu.SMEM((2,), jnp.int32),
+                dma((7,)),
                 dma((HOPS, 2)),
                 dma((HOPS, 2, 2)),
                 dma((HOPS, 2, 2)),
                 dma((groups - 1,)),
                 dma((groups - 1,)),
+                pltpu.SemaphoreType.REGULAR((2,)),
             ],
             compiler_params=pltpu.CompilerParams(
-                collective_id=0, has_side_effects=True, vmem_limit_bytes=56 * 1024 * 1024
+                collective_id=0, has_side_effects=True, vmem_limit_bytes=40 * 1024 * 1024
             ),
-        )(screen_values, freq_index, down_state, up_state, source, reflect, screen_class, table)
+        )(
+            *(
+                pltpu.with_memory_space_constraint(x, pltpu.HBM)
+                for x in (
+                    screen_values,
+                    freq_index,
+                    down_state,
+                    up_state,
+                    source,
+                    reflect,
+                    screen_class,
+                    table,
+                )
+            ),
+        )
+        return pl.pallas_call(
+            store,
+            out_shape=[pltpu.HBM(x.shape, x.dtype) for x in results],
+            in_specs=[vmem] * 3,
+            out_specs=[hbm] * 3,
+            scratch_shapes=[dma((3,))],
+        )(*(pltpu.with_memory_space_constraint(x, pltpu.VMEM) for x in results))
 
     return jax.shard_map(
         per_device,

time: 47.9 us -> 42.7 us (0.89)
  local copies, waits for them, and re-layouts: 3.96 us -> 0 us
  Pallas kernels: 43.1 us -> 41.9 us
    unnamed x7 -> x0, local copies, waits for them, and re-layouts: 3.96 us -> none
    pallas_call x1 -> x2, Pallas kernels: 43.1 us -> 41.9 us  [the longest x1 40.6 us: per_device(): pl.pallas_call(lambda *refs: kernel(groups, slabs, *refs), out_shape=(plt...]
where the time goes in v2:
time: 42.7 us; the launch traced here: 42.6 us
  Pallas kernels  41.9 us (98%)
  between operations  0.64 us (1%)
    pallas_call x1, Pallas kernels, per_device(): pl.pallas_call(lambda *refs: kernel(groups, slabs, *refs), out_shape=(plt...  40.6 us
    pallas_call x1, Pallas kernels, per_device(): pl.pallas_call(store, out_shape=[pltpu.HBM(x.shape, x.dtype) for x in res...  1.35 us

profile of v2, /device:TPU:24, one launch (start us, length us, event | category | flops | bytes accessed | tf_op | source)
XLA Modules:
  0.0 42.6 jit_solution(10126983221179544658)
XLA Ops:
  0.6 40.6 %shard_map.103 = (bf16[2,2,2,256,256]{4,3,2,1,0:T(8,128)(2,1)S(1)}, bf16[2,2,2,256,256]{4,3,2,1,0:T(8,128)(2,1)S(1)}, f32[2,32,256]{2,1,0:T(8,128)S(1)}) custom-call(f32[16]{0:T(128)} %refs_0_.1, s32[2]{0:T(128)} %refs_1_.1, bf16[2,2,2,256,256]{4,3,2,1,0:T(8,128)(2,1)} %refs_2_.1, bf16[2,2,2,256,256]{4,3,2,1,0:T(8,128)(2,1)} %refs_3_.1, ...), custom_call_target="tpu_custom_call" | custom-call | tf_op jit(solution)/shard_map/pallas_call | solution.py:434
  41.2 1.3 %shard_map.104 = (bf16[2,2,2,256,256]{4,3,2,1,0:T(8,128)(2,1)}, bf16[2,2,2,256,256]{4,3,2,1,0:T(8,128)(2,1)}, f32[2,32,256]{2,1,0:T(8,128)}) custom-call(bf16[2,2,2,256,256]{4,3,2,1,0:T(8,128)(2,1)S(1)} %get-tuple-element.6.refs_0_, bf16[2,2,2,256,256]{4,3,2,1,0:T(8,128)(2,1)S(1)} %get-tuple-element.7.refs_1_, f32[2,32,256]{2,1,0:T(8,128)S(1)} %get-tuple-element.8.refs_2_), custom_call_target="tpu_custom_call" | custom-call | tf_op jit(solution)/shard_map/pallas_call | solution.py:488

commit v3 on v2

v3 whole, which is shorter than its diff:
```python
import math

import jax
import jax.numpy as jnp
import numpy as np
from jax import lax
from jax.experimental import pallas as pl
from jax.experimental.pallas import tpu as pltpu
from jax.sharding import PartitionSpec as P

HOPS = 3
NCLASS = 16
NFREQ = 128
N = 256
H = N // 2
MESH = pl.DeviceIdType.MESH
BF16 = jnp.bfloat16
F32 = jnp.float32
COS_COEFS = [(-1.0) ** k / math.factorial(2 * k) for k in range(10)]
SIN_COEFS = [(-1.0) ** k / math.factorial(2 * k + 1) for k in range(10)]


def half_tables():
    row = np.arange(H)[:, None]
    col = np.arange(H)[None, :]
    mats = []
    for parity in (0, 1):
        angle = (2.0 * math.pi / N) * (((2 * row + parity) * col) % N).astype(np.float64)
        cos, sin = np.cos(angle), np.sin(angle)
        fwd = np.block([[cos, sin], [-sin, cos]])
        mats.append(fwd)
        mats.append(fwd.T)
    return np.stack(mats).astype(np.float32)


def poly(coefs, q):
    acc = jnp.full_like(q, coefs[-1])
    for c in coefs[-2::-1]:
        acc = acc * q + c
    return acc


def dot(a, b):
    return jnp.dot(a, b, preferred_element_type=F32)


def kernel(
    groups,
    slabs,
    values_hbm,
    freq_hbm,
    down_hbm,
    up_hbm,
    source_hbm,
    reflect_hbm,
    class_hbm,
    table_hbm,
    local,
    edge,
    grad_out,
    tab,
    classes,
    refl,
    halo,
    inner,
    phase,
    screen,
    lut,
    s2,
    s3,
    s4,
    gsum,
    gsend,
    grecv,
    screen_values,
    freq_index,
    load_sem,
    src_sem,
    send_sem,
    recv_sem,
    gsend_sem,
    grecv_sem,
    near_sem,
):
    d = lax.axis_index("depth")
    s = lax.axis_index("shot")
    has_above = d > 0
    has_below = d < slabs - 1

    loads = [
        pltpu.make_async_copy(table_hbm, tab, load_sem.at[0]),
        pltpu.make_async_copy(class_hbm, classes, load_sem.at[1]),
        pltpu.make_async_copy(reflect_hbm, refl, load_sem.at[2]),
        pltpu.make_async_copy(down_hbm.at[0], local.at[0], load_sem.at[3]),
        pltpu.make_async_copy(up_hbm.at[1], local.at[1], load_sem.at[4]),
        pltpu.make_async_copy(freq_hbm, freq_index, load_sem.at[5]),
        pltpu.make_async_copy(values_hbm, screen_values, load_sem.at[6]),
    ]
    near = [
        lax.rem(s + 2, groups),
        lax.rem(s + groups - 2, groups),
        s + 1 - 2 * lax.rem(s, 2),
    ]

    def greet(sem):
        for peer in near:
            pl.semaphore_signal(sem, inc=1, device_id={"shot": peer}, device_id_type=MESH)

    barrier = pltpu.get_barrier_semaphore()

    @pl.when(has_above)
    def _():
        pl.semaphore_signal(barrier, inc=1, device_id={"depth": d - 1}, device_id_type=MESH)

    @pl.when(has_below)
    def _():
        pl.semaphore_signal(barrier, inc=1, device_id={"depth": d + 1}, device_id_type=MESH)

    greet(barrier)
    for c in loads[::-1]:
        c.start()

    def link(src, h, k, f):
        return pltpu.make_async_remote_copy(
            src_ref=src,
            dst_ref=halo.at[h, 1 - k, f],
            send_sem=send_sem.at[h, k, f],
            recv_sem=recv_sem.at[h, 1 - k, f],
            device_id={"depth": lax.rem(d + 2 * k + slabs - 1, slabs)},
            device_id_type=MESH,
        )

    def linked(k):
        peer = d + 2 * k - 1
        return jnp.logical_and(peer >= 0, peer < slabs)

    def from_source(h, f):
        return pltpu.make_async_copy(source_hbm.at[f], halo.at[h, 0, f], src_sem.at[h, f])

    late = lax.rem(d, 2)
    early = 1 - late

    def fill_phase(f):
        k0 = 0.95 * math.pi * (freq_index[f].astype(F32) + 1.0) / NFREQ

        def rows(t, carry):
            r0 = pl.multiple_of(t * 8, 8)
            row = lax.broadcasted_iota(jnp.int32, (8, N), 0) + r0
            lane = lax.broadcasted_iota(jnp.int32, (8, N), 1)
            ym = jnp.where(lane < H, 2 * lane, 2 * (lane - H) + 1)
            ym = jnp.where(ym >= H, ym - N, ym)
            ky = (2.0 * math.pi / N) * ym.astype(F32)
            for par in range(2):
                xm = 2 * row + par
                xm = jnp.where(xm >= H, xm - N, xm)
                kx = (2.0 * math.pi / N) * xm.astype(F32)
                q = k0 * k0 - (kx * kx + ky * ky)
                root = jnp.sqrt(jnp.abs(q))
                qp = jnp.maximum(q, 0.0)
                damp = jnp.where(q < 0.0, jnp.exp(-root), 1.0) * (1.0 / (N * N))
                sin = jnp.where(q > 0.0, root, 0.0) * poly(SIN_COEFS, qp)
                phase[f, par, 0, pl.ds(r0, 8), :] = damp * poly(COS_COEFS, qp)
                phase[f, par, 1, pl.ds(r0, 8), :] = damp * sin
            return carry

        lax.fori_loop(0, H // 8, rows, 0)

    def fill_screen(f):
        k0 = 0.95 * math.pi * (freq_index[f].astype(F32) + 1.0) / NFREQ
        for c in range(NCLASS):
            ang = jnp.full((8, 128), k0 * screen_values[c], F32)
            q = ang * ang
            lut[0, c] = poly(COS_COEFS, q)
            lut[1, c] = ang * poly(SIN_COEFS, q)

        def rows(t, carry):
            lev = t // (N // 8)
            r0 = pl.multiple_of(lax.rem(t, N // 8) * 8, 8)
            cls = [classes[lev, pl.ds(r0, 8), pl.ds(j * H, H)] for j in range(2)]
            bits = [[(c & (1 << b)) != 0 for b in range(4)] for c in cls]
            for k in range(2):
                table = [lut[k, c] for c in range(NCLASS)]
                for j in range(2):
                    vals = table
                    for b in range(4):
                        vals = [
                            jnp.where(bits[j][b], vals[2 * i + 1], vals[2 * i])
                            for i in range(len(vals) // 2)
                        ]
                    screen[lev, f, k, pl.ds(r0, 8), pl.ds(j * H, H)] = vals[0]
            return carry

        lax.fori_loop(0, 2 * N // 8, rows, 0)

    loads[5].wait()
    fill_phase(0)
    pl.semaphore_wait(
        barrier, len(near) + has_above.astype(jnp.int32) + has_below.astype(jnp.int32)
    )

    for f in range(2):

        @pl.when(has_above)
        def _():
            link(up_hbm.at[0, f], 0, 0, f).start()

        @pl.when(has_below)
        def _():
            link(down_hbm.at[1, f], 0, 1, f).start()

    @pl.when(jnp.logical_not(has_above))
    def _():
        for h in range(HOPS):
            for f in range(2):
                from_source(h, f).start()

    @pl.when(jnp.logical_not(has_below))
    def _():
        def clear(t, carry):
            halo[t // 2, 1, lax.rem(t, 2)] = jnp.zeros((2, N, N), BF16)
            return carry

        lax.fori_loop(0, 2 * HOPS, clear, 0)

    greet(near_sem.at[0])

    def propagate(srcs, f):
        fe, ie, fo, io = 0, 1, 2, 3
        n = len(srcs)
        sums, difs = [], []
        for src in srcs:
            re_l, re_r = src[0, :, :H], src[0, :, H:]
            im_l, im_r = src[1, :, :H], src[1, :, H:]
            sums.append(jnp.concatenate([re_l + re_r, im_l + im_r], axis=1))
            difs.append(jnp.concatenate([re_l - re_r, im_l - im_r], axis=1))
        ev = dot(jnp.concatenate(sums, axis=0), tab[ie])
        od = dot(jnp.concatenate(difs, axis=0), tab[io])
        for i in range(n):
            for j, x in enumerate((ev[i * N : (i + 1) * N], od[i * N : (i + 1) * N])):
                cols = slice(j * H, (j + 1) * H)
                u = (x[:H] + x[H:]).astype(BF16)
                v = (x[:H] - x[H:]).astype(BF16)
                s2[i, 0, :H, cols] = u[:, :H]
                s2[i, 0, H:, cols] = u[:, H:]
                s2[i, 1, :H, cols] = v[:, :H]
                s2[i, 1, H:, cols] = v[:, H:]
        for i in range(n):
            for par, t in enumerate((fe, fo)):
                x = dot(tab[t], s2[i, par])
                pr, pi = phase[f, par, 0], phase[f, par, 1]
                re, im = x[:H], x[H:]
                s3[i, par, :H] = (re * pr - im * pi).astype(BF16)
                s3[i, par, H:] = (re * pi + im * pr).astype(BF16)
        for i in range(n):
            e = dot(tab[ie], s3[i, 0])
            o = dot(tab[io], s3[i, 1])
            top = (e + o).astype(BF16)
            bot = (e - o).astype(BF16)
            lo, hi = slice(i * N, i * N + H), slice(i * N + H, i * N + N)
            for j in range(2):
                cols = slice(j * H, (j + 1) * H)
                s4[j, lo, :H] = top[:H, cols]
                s4[j, lo, H:] = top[H:, cols]
                s4[j, hi, :H] = bot[:H, cols]
                s4[j, hi, H:] = bot[H:, cols]
        e = dot(s4[0, : n * N], tab[fe])
        o = dot(s4[1, : n * N], tab[fo])
        sm, df = e + o, e - o
        return [(sm[i * N : (i + 1) * N], df[i * N : (i + 1) * N]) for i in range(n)]

    def screened(x, lev, f, j):
        cols = slice(j * H, (j + 1) * H)
        sr, si = screen[lev, f, 0, :, cols], screen[lev, f, 1, :, cols]
        re, im = x[j][:, :H], x[j][:, H:]
        return (sr * re - si * im, sr * im + si * re)

    def inner_step(f):
        for i, q in enumerate(propagate((local.at[0, f], local.at[1, f]), f)):
            for j in range(2):
                cols = slice(j * H, (j + 1) * H)
                for c, x in enumerate(screened(q, 1 - i, f, j)):
                    inner[1 - i, f, c, :, cols] = x

    rows = N // groups
    scale = 1.0 / math.sqrt(2 * groups)

    def wait_halo(h, k, f):
        @pl.when(linked(k))
        def _():
            link(halo.at[h, k, f], h, 1 - k, f).wait_recv()

        @pl.when(jnp.logical_and(d == 0, k == 0))
        def _():
            from_source(h, f).wait()

    def meet(q, h, k, f, grad):
        for j in range(2):
            cols = slice(j * H, (j + 1) * H)
            r = refl[k, :, cols]
            xs = screened(q, k, f, j)
            g = None
            for c in range(2):
                x, y = xs[c], inner[k, f, c, :, cols]
                t = r * (x - y)
                edge[h, k, f, c, :, cols] = (y + t).astype(BF16)
                local[k, f, c, :, cols] = (x + t).astype(BF16)
                g = x * y if g is None else g + x * y
            if grad == "keep":
                gsum[k, :, cols] = g
            elif grad == "share":
                out = ((gsum[k, :, cols] + g) * scale).astype(BF16)
                for p in range(groups):
                    gsend[k, p, :, cols] = out[p * rows : (p + 1) * rows]

    def send(h, k, f):
        @pl.when(linked(k))
        def _():
            link(edge.at[h, k, f], h + 1, k, f).start()

    mate = s + 1 - 2 * lax.rem(s, 2)

    def over(p, o):
        return lax.rem(p + o, groups)

    peers = [over(mate, 4), over(mate, 2), over(mate, 6), over(s, 4), mate, over(s, 2), over(s, 6)]

    def share(k, i):
        return pltpu.make_async_remote_copy(
            src_ref=gsend.at[k, peers[i]],
            dst_ref=grecv.at[k, i],
            send_sem=gsend_sem.at[k, i],
            recv_sem=grecv_sem.at[k, i],
            device_id={"shot": peers[i]},
            device_id_type=MESH,
        )

    loads[6].wait()
    loads[1].wait()
    loads[2].wait()
    fill_screen(0)
    refl[1] = -refl[1]
    loads[0].wait()
    loads[3].wait()
    loads[4].wait()

    def first(f, carry):
        @pl.when(f == 1)
        def _():
            fill_phase(1)
            fill_screen(1)

        inner_step(f)
        return carry

    lax.fori_loop(0, 2, first, 0)
    pl.semaphore_wait(near_sem.at[0], len(near))
    greet(near_sem.at[1])

    def pair(h, f):
        wait_halo(h, early, f)
        wait_halo(h, late, f)
        return propagate((halo.at[h, late, f], halo.at[h, early, f]), f)

    def middle(t, carry):
        h, f = t // 2, lax.rem(t, 2)
        ql, qe = pair(h, f)
        meet(ql, h, late, f, None)
        send(h, late, f)
        meet(qe, h, early, f, None)
        send(h, early, f)
        inner_step(f)
        return carry

    lax.fori_loop(0, 2 * (HOPS - 1), middle, 0)
    pl.semaphore_wait(near_sem.at[1], len(near))

    end = HOPS - 1
    ql, qe = pair(end, 0)
    meet(ql, end, late, 0, "keep")
    meet(qe, end, early, 0, "keep")

    def final(t, carry):
        k = early + t * (late - early)
        wait_halo(end, k, 1)
        (q,) = propagate((halo.at[end, k, 1],), 1)
        meet(q, end, k, 1, "share")
        for i in range(groups - 1):
            share(k, i).start()
        return carry

    lax.fori_loop(0, 2, final, 0)

    for h in range(HOPS):
        for k in range(2):
            for f in range(2):

                @pl.when(linked(k))
                def _():
                    link(edge.at[0, k, f], h, k, f).wait_send()

    for k in (early, late):
        total = gsend[k, s].astype(F32)
        for i in range(groups - 1):
            share(k, i).wait_recv()
            total = total + grecv[k, i].astype(F32)
        grad_out[k] = total
    for k in range(2):
        for i in range(groups - 1):
            share(k, i).wait_send()


def store(local, edge, grad, down_out, up_out, grad_out, sems):
    last = edge.shape[0] - 1
    pairs = [
        (local.at[0], down_out.at[0]),
        (edge.at[last, 1], down_out.at[1]),
        (edge.at[last, 0], up_out.at[0]),
        (local.at[1], up_out.at[1]),
        (grad, grad_out),
    ]
    copies = [pltpu.make_async_copy(a, b, sems.at[i]) for i, (a, b) in enumerate(pairs)]
    for c in copies:
        c.start()
    for c in copies:
        c.wait()


def solution(mesh):
    groups = mesh.shape["shot"]
    slabs = mesh.shape["depth"]
    rows = N // groups

    def per_device(down_state, up_state, source, reflect, screen_class, screen_values, freq_index):
        table = jnp.asarray(half_tables(), BF16)
        hbm = pl.BlockSpec(memory_space=pltpu.HBM)
        vmem = pl.BlockSpec(memory_space=pltpu.VMEM)
        dma = pltpu.SemaphoreType.DMA
        results = pl.pallas_call(
            lambda *refs: kernel(groups, slabs, *refs),
            out_shape=(
                pltpu.VMEM((2, 2, 2, N, N), BF16),
                pltpu.VMEM((HOPS, 2, 2, 2, N, N), BF16),
                pltpu.VMEM((2, rows, N), F32),
            ),
            in_specs=[hbm] * 8,
            out_specs=(vmem, vmem, vmem),
            scratch_shapes=[
                pltpu.VMEM((4, N, N), BF16),
                pltpu.VMEM((2, N, N), jnp.int32),
                pltpu.VMEM((2, N, N), F32),
                pltpu.VMEM((HOPS, 2, 2, 2, N, N), BF16),
                pltpu.VMEM((2, 2, 2, N, N), F32),
                pltpu.VMEM((2, 2, 2, H, N), F32),
                pltpu.VMEM((2, 2, 2, N, N), F32),
                pltpu.VMEM((2, NCLASS, 8, 128), F32),
                pltpu.VMEM((2, 2, N, N), BF16),
                pltpu.VMEM((2, 2, N, N), BF16),
                pltpu.VMEM((2, 2 * N, N), BF16),
                pltpu.VMEM((2, N, N), F32),
                pltpu.VMEM((2, groups, rows, N), BF16),
                pltpu.VMEM((2, groups - 1, rows, N), BF16),
                pltpu.SMEM((NCLASS,), F32),
                pltpu.SMEM((2,), jnp.int32),
                dma((7,)),
                dma((HOPS, 2)),
                dma((HOPS, 2, 2)),
                dma((HOPS, 2, 2)),
                dma((2, groups - 1)),
                dma((2, groups - 1)),
                pltpu.SemaphoreType.REGULAR((2,)),
            ],
            compiler_params=pltpu.CompilerParams(
                collective_id=0, has_side_effects=True, vmem_limit_bytes=40 * 1024 * 1024
            ),
        )(
            *(
                pltpu.with_memory_space_constraint(x, pltpu.HBM)
                for x in (
                    screen_values,
                    freq_index,
                    down_state,
                    up_state,
                    source,
                    reflect,
                    screen_class,
                    table,
                )
            ),
        )
        return pl.pallas_call(
            store,
            out_shape=[
                pltpu.HBM(down_state.shape, BF16),
                pltpu.HBM(up_state.shape, BF16),
                pltpu.HBM((2, rows, N), F32),
            ],
            in_specs=[vmem] * 3,
            out_specs=[hbm] * 3,
            scratch_shapes=[dma((5,))],
            compiler_params=pltpu.CompilerParams(vmem_limit_bytes=1024 * 1024),
        )(*(pltpu.with_memory_space_constraint(x, pltpu.VMEM) for x in results))

    return jax.shard_map(
        per_device,
        mesh=mesh,
        in_specs=(
            P("depth", "shot", None, None, None),
            P("depth", "shot", None, None, None),
            P("shot", None, None, None),
            P("depth", None, None),
            P("depth", None, None),
            P(),
            P("shot"),
        ),
        out_specs=(
            P("depth", "shot", None, None, None),
            P("depth", "shot", None, None, None),
            P("depth", "shot", None),
        ),
        check_vma=False,
    )
```

time: 42.7 us -> 41 us (0.960)
  Pallas kernels: 41.9 us -> 40.3 us
    pallas_call x1, Pallas kernels: 40.6 us -> 38.9 us  [per_device(): pl.pallas_call(lambda *refs: kernel(groups, slabs, *refs), out_shape=(plt...]
where the time goes in v3:
time: 41 us; the launch traced here: 40.9 us
  Pallas kernels  40.3 us (98%)
  between operations  0.64 us (2%)
    pallas_call x1, Pallas kernels, per_device(): pl.pallas_call(lambda *refs: kernel(groups, slabs, *refs), out_shape=(plt...  38.9 us
    pallas_call x1, Pallas kernels, per_device(): pl.pallas_call(store, out_shape=[pltpu.HBM(down_state.shape, BF16), pltpu...  1.37 us

profile of v3, /device:TPU:24, one launch (start us, length us, event | category | flops | bytes accessed | tf_op | source)
XLA Modules:
  0.0 40.9 jit_solution(3621743585490266172)
XLA Ops:
  0.6 38.9 %shard_map.103 = (bf16[2,2,2,256,256]{4,3,2,1,0:T(8,128)(2,1)S(1)}, bf16[3,2,2,2,256,256]{5,4,3,2,1,0:T(8,128)(2,1)S(1)}, f32[2,32,256]{2,1,0:T(8,128)S(1)}) custom-call(f32[16]{0:T(128)} %refs_0_.1, s32[2]{0:T(128)} %refs_1_.1, bf16[2,2,2,256,256]{4,3,2,1,0:T(8,128)(2,1)} %refs_2_.1, bf16[2,2,2,256,256]{4,3,2,1,0:T(8,128)(2,1)} %refs_3_.1, ...), custom_call_target="tpu_custom_call" | custom-call | tf_op jit(solution)/shard_map/pallas_call | solution.py:438
  39.5 1.4 %shard_map.104 = (bf16[2,2,2,256,256]{4,3,2,1,0:T(8,128)(2,1)}, bf16[2,2,2,256,256]{4,3,2,1,0:T(8,128)(2,1)}, f32[2,32,256]{2,1,0:T(8,128)}) custom-call(bf16[2,2,2,256,256]{4,3,2,1,0:T(8,128)(2,1)S(1)} %get-tuple-element.6.local, bf16[3,2,2,2,256,256]{5,4,3,2,1,0:T(8,128)(2,1)S(1)} %get-tuple-element.7.edge, f32[2,32,256]{2,1,0:T(8,128)S(1)} %get-tuple-element.8.grad), custom_call_target="tpu_custom_call" | custom-call | tf_op jit(solution)/shard_map/pallas_call | solution.py:490

commit v4 on v3

--- a/solution.py
+++ b/solution.py
@@ -70,6 +70,7 @@
     s3,
     s4,
     gsum,
+    final_x,
     gsend,
     grecv,
     screen_values,
@@ -140,30 +141,27 @@
     late = lax.rem(d, 2)
     early = 1 - late
 
-    def fill_phase(f):
-        k0 = 0.95 * math.pi * (freq_index[f].astype(F32) + 1.0) / NFREQ
-
-        def rows(t, carry):
-            r0 = pl.multiple_of(t * 8, 8)
-            row = lax.broadcasted_iota(jnp.int32, (8, N), 0) + r0
-            lane = lax.broadcasted_iota(jnp.int32, (8, N), 1)
-            ym = jnp.where(lane < H, 2 * lane, 2 * (lane - H) + 1)
-            ym = jnp.where(ym >= H, ym - N, ym)
-            ky = (2.0 * math.pi / N) * ym.astype(F32)
-            for par in range(2):
-                xm = 2 * row + par
-                xm = jnp.where(xm >= H, xm - N, xm)
-                kx = (2.0 * math.pi / N) * xm.astype(F32)
-                q = k0 * k0 - (kx * kx + ky * ky)
+    def fill_phase(t, carry):
+        r0 = pl.multiple_of(t * 8, 8)
+        row = lax.broadcasted_iota(jnp.int32, (8, N), 0) + r0
+        lane = lax.broadcasted_iota(jnp.int32, (8, N), 1)
+        ym = jnp.where(lane < H, 2 * lane, 2 * (lane - H) + 1)
+        ym = jnp.where(ym >= H, ym - N, ym)
+        ky = (2.0 * math.pi / N) * ym.astype(F32)
+        for par in range(2):
+            xm = 2 * row + par
+            xm = jnp.where(xm >= H, xm - N, xm)
+            kx = (2.0 * math.pi / N) * xm.astype(F32)
+            k2 = kx * kx + ky * ky
+            for f in range(2):
+                q = kwave[f] * kwave[f] - k2
                 root = jnp.sqrt(jnp.abs(q))
                 qp = jnp.maximum(q, 0.0)
                 damp = jnp.where(q < 0.0, jnp.exp(-root), 1.0) * (1.0 / (N * N))
                 sin = jnp.where(q > 0.0, root, 0.0) * poly(SIN_COEFS, qp)
                 phase[f, par, 0, pl.ds(r0, 8), :] = damp * poly(COS_COEFS, qp)
                 phase[f, par, 1, pl.ds(r0, 8), :] = damp * sin
-            return carry
-
-        lax.fori_loop(0, H // 8, rows, 0)
+        return carry
 
     def fill_screen(f):
         k0 = 0.95 * math.pi * (freq_index[f].astype(F32) + 1.0) / NFREQ
@@ -174,26 +172,29 @@
             lut[1, c] = ang * poly(SIN_COEFS, q)
 
         def rows(t, carry):
-            lev = t // (N // 8)
-            r0 = pl.multiple_of(lax.rem(t, N // 8) * 8, 8)
-            cls = [classes[lev, pl.ds(r0, 8), pl.ds(j * H, H)] for j in range(2)]
-            bits = [[(c & (1 << b)) != 0 for b in range(4)] for c in cls]
-            for k in range(2):
-                table = [lut[k, c] for c in range(NCLASS)]
+            lev = t // (N // 32)
+            r0 = pl.multiple_of(lax.rem(t, N // 32) * 32, 32)
+            tables = [[lut[k, c] for c in range(NCLASS)] for k in range(2)]
+            for i in range(4):
                 for j in range(2):
-                    vals = table
-                    for b in range(4):
-                        vals = [
-                            jnp.where(bits[j][b], vals[2 * i + 1], vals[2 * i])
-                            for i in range(len(vals) // 2)
-                        ]
-                    screen[lev, f, k, pl.ds(r0, 8), pl.ds(j * H, H)] = vals[0]
+                    here = (pl.ds(r0 + 8 * i, 8), pl.ds(j * H, H))
+                    cls = classes[lev, *here]
+                    bits = [(cls & (1 << b)) != 0 for b in range(4)]
+                    for k in range(2):
+                        vals = tables[k]
+                        for bit in bits:
+                            vals = [
+                                jnp.where(bit, vals[2 * m + 1], vals[2 * m])
+                                for m in range(len(vals) // 2)
+                            ]
+                        screen[lev, f, k, *here] = vals[0]
             return carry
 
-        lax.fori_loop(0, 2 * N // 8, rows, 0)
+        lax.fori_loop(0, 2 * N // 32, rows, 0)
 
     loads[5].wait()
-    fill_phase(0)
+    kwave = [0.95 * math.pi * (freq_index[f].astype(F32) + 1.0) / NFREQ for f in range(2)]
+    lax.fori_loop(0, H // 8, fill_phase, 0)
     pl.semaphore_wait(
         barrier, len(near) + has_above.astype(jnp.int32) + has_below.astype(jnp.int32)
     )
@@ -293,7 +294,7 @@
         def _():
             from_source(h, f).wait()
 
-    def meet(q, h, k, f, grad):
+    def meet(q, h, k, f, keep):
         for j in range(2):
             cols = slice(j * H, (j + 1) * H)
             r = refl[k, :, cols]
@@ -305,12 +306,26 @@
                 edge[h, k, f, c, :, cols] = (y + t).astype(BF16)
                 local[k, f, c, :, cols] = (x + t).astype(BF16)
                 g = x * y if g is None else g + x * y
-            if grad == "keep":
+            if keep:
                 gsum[k, :, cols] = g
-            elif grad == "share":
-                out = ((gsum[k, :, cols] + g) * scale).astype(BF16)
-                for p in range(groups):
-                    gsend[k, p, :, cols] = out[p * rows : (p + 1) * rows]
+
+    def meet_last(q, h, k, f):
+        for j in range(2):
+            cols = slice(j * H, (j + 1) * H)
+            re, im = screened(q, k, f, j)
+            final_x[0, :, cols] = re
+            final_x[1, :, cols] = im
+            g = re * inner[k, f, 0, :, cols] + im * inner[k, f, 1, :, cols]
+            out = ((gsum[k, :, cols] + g) * scale).astype(BF16)
+            for p in range(groups):
+                gsend[k, p, :, cols] = out[p * rows : (p + 1) * rows]
+        for i in range(groups - 1):
+            share(k, i).start()
+        for c in range(2):
+            x, y = final_x[c], inner[k, f, c]
+            t = refl[k] * (x - y)
+            edge[h, k, f, c] = (y + t).astype(BF16)
+            local[k, f, c] = (x + t).astype(BF16)
 
     def send(h, k, f):
         @pl.when(linked(k))
@@ -346,7 +361,6 @@
     def first(f, carry):
         @pl.when(f == 1)
         def _():
-            fill_phase(1)
             fill_screen(1)
 
         inner_step(f)
@@ -364,9 +378,9 @@
     def middle(t, carry):
         h, f = t // 2, lax.rem(t, 2)
         ql, qe = pair(h, f)
-        meet(ql, h, late, f, None)
+        meet(ql, h, late, f, False)
         send(h, late, f)
-        meet(qe, h, early, f, None)
+        meet(qe, h, early, f, False)
         send(h, early, f)
         inner_step(f)
         return carry
@@ -376,16 +390,14 @@
 
     end = HOPS - 1
     ql, qe = pair(end, 0)
-    meet(ql, end, late, 0, "keep")
-    meet(qe, end, early, 0, "keep")
+    meet(ql, end, late, 0, True)
+    meet(qe, end, early, 0, True)
 
     def final(t, carry):
         k = early + t * (late - early)
         wait_halo(end, k, 1)
         (q,) = propagate((halo.at[end, k, 1],), 1)
-        meet(q, end, k, 1, "share")
-        for i in range(groups - 1):
-            share(k, i).start()
+        meet_last(q, end, k, 1)
         return carry
 
     lax.fori_loop(0, 2, final, 0)
@@ -456,6 +468,7 @@
                 pltpu.VMEM((2, 2, N, N), BF16),
                 pltpu.VMEM((2, 2, N, N), BF16),
                 pltpu.VMEM((2, 2 * N, N), BF16),
+                pltpu.VMEM((2, N, N), F32),
                 pltpu.VMEM((2, N, N), F32),
                 pltpu.VMEM((2, groups, rows, N), BF16),
                 pltpu.VMEM((2, groups - 1, rows, N), BF16),

time: 41 us -> 41 us (level); the launches traced: 40.9 us -> 40.4 us
  Pallas kernels: 40.3 us -> 39.7 us
    pallas_call x1, Pallas kernels: 38.9 us -> 38.3 us  [per_device(): pl.pallas_call(lambda *refs: kernel(groups, slabs, *refs), out_shape=(plt...]
where the time goes in v4:
time: 41 us; the launch traced here: 40.4 us
  Pallas kernels  39.7 us (97%)
  between operations  0.64 us (2%)
    pallas_call x1, Pallas kernels, per_device(): pl.pallas_call(lambda *refs: kernel(groups, slabs, *refs), out_shape=(plt...  38.3 us
    pallas_call x1, Pallas kernels, per_device(): pl.pallas_call(store, out_shape=[pltpu.HBM(down_state.shape, BF16), pltpu...  1.37 us

profile of v4, /device:TPU:24, one launch (start us, length us, event | category | flops | bytes accessed | tf_op | source)
XLA Modules:
  0.0 40.4 jit_solution(11422052797207787138)
XLA Ops:
  0.6 38.3 %shard_map.103 = (bf16[2,2,2,256,256]{4,3,2,1,0:T(8,128)(2,1)S(1)}, bf16[3,2,2,2,256,256]{5,4,3,2,1,0:T(8,128)(2,1)S(1)}, f32[2,32,256]{2,1,0:T(8,128)S(1)}) custom-call(f32[16]{0:T(128)} %refs_0_.1, s32[2]{0:T(128)} %refs_1_.1, bf16[2,2,2,256,256]{4,3,2,1,0:T(8,128)(2,1)} %refs_2_.1, bf16[2,2,2,256,256]{4,3,2,1,0:T(8,128)(2,1)} %refs_3_.1, ...), custom_call_target="tpu_custom_call" | custom-call | tf_op jit(solution)/shard_map/pallas_call | solution.py:450
  39.0 1.4 %shard_map.104 = (bf16[2,2,2,256,256]{4,3,2,1,0:T(8,128)(2,1)}, bf16[2,2,2,256,256]{4,3,2,1,0:T(8,128)(2,1)}, f32[2,32,256]{2,1,0:T(8,128)}) custom-call(bf16[2,2,2,256,256]{4,3,2,1,0:T(8,128)(2,1)S(1)} %get-tuple-element.6.local, bf16[3,2,2,2,256,256]{5,4,3,2,1,0:T(8,128)(2,1)S(1)} %get-tuple-element.7.edge, f32[2,32,256]{2,1,0:T(8,128)S(1)} %get-tuple-element.8.grad), custom_call_target="tpu_custom_call" | custom-call | tf_op jit(solution)/shard_map/pallas_call | solution.py:503

commit v5 on v4

--- a/solution.py
+++ b/solution.py
@@ -138,6 +138,8 @@
     def from_source(h, f):
         return pltpu.make_async_copy(source_hbm.at[f], halo.at[h, 0, f], src_sem.at[h, f])
 
+    turn = slabs // 2
+    holds = d == turn + 1
     late = lax.rem(d, 2)
     early = 1 - late
 
@@ -319,8 +321,12 @@
             out = ((gsum[k, :, cols] + g) * scale).astype(BF16)
             for p in range(groups):
                 gsend[k, p, :, cols] = out[p * rows : (p + 1) * rows]
-        for i in range(groups - 1):
-            share(k, i).start()
+
+        @pl.when(jnp.logical_not(holds))
+        def _():
+            for i in range(groups - 1):
+                share(k, i).start()
+
         for c in range(2):
             x, y = final_x[c], inner[k, f, c]
             t = refl[k] * (x - y)
@@ -396,11 +402,25 @@
     def final(t, carry):
         k = early + t * (late - early)
         wait_halo(end, k, 1)
+
+        @pl.when(jnp.logical_and(d == turn, t == 1))
+        def _():
+            pl.semaphore_signal(
+                near_sem.at[2], inc=1, device_id={"depth": d + 1}, device_id_type=MESH
+            )
+
         (q,) = propagate((halo.at[end, k, 1],), 1)
         meet_last(q, end, k, 1)
         return carry
 
     lax.fori_loop(0, 2, final, 0)
+
+    @pl.when(holds)
+    def _():
+        pl.semaphore_wait(near_sem.at[2], 1)
+        for k in range(2):
+            for i in range(groups - 1):
+                share(k, i).start()
 
     for h in range(HOPS):
         for k in range(2):
@@ -480,7 +500,7 @@
                 dma((HOPS, 2, 2)),
                 dma((2, groups - 1)),
                 dma((2, groups - 1)),
-                pltpu.SemaphoreType.REGULAR((2,)),
+                pltpu.SemaphoreType.REGULAR((3,)),
             ],
             compiler_params=pltpu.CompilerParams(
                 collective_id=0, has_side_effects=True, vmem_limit_bytes=40 * 1024 * 1024

time: 41 us -> 41.3 us (level)
  no operation moved by 1% of the time
where the time goes in v5:
time: 41.3 us; the launch traced here: 40.5 us
  Pallas kernels  39.9 us (97%)
  between operations  0.64 us (2%)
    pallas_call x1, Pallas kernels, per_device(): pl.pallas_call(lambda *refs: kernel(groups, slabs, *refs), out_shape=(plt...  38.5 us
    pallas_call x1, Pallas kernels, per_device(): pl.pallas_call(store, out_shape=[pltpu.HBM(down_state.shape, BF16), pltpu...  1.37 us

profile of v5, /device:TPU:24, one launch (start us, length us, event | category | flops | bytes accessed | tf_op | source)
XLA Modules:
  0.0 40.5 jit_solution(10966668036467255656)
XLA Ops:
  0.6 38.5 %shard_map.103 = (bf16[2,2,2,256,256]{4,3,2,1,0:T(8,128)(2,1)S(1)}, bf16[3,2,2,2,256,256]{5,4,3,2,1,0:T(8,128)(2,1)S(1)}, f32[2,32,256]{2,1,0:T(8,128)S(1)}) custom-call(f32[16]{0:T(128)} %refs_0_.1, s32[2]{0:T(128)} %refs_1_.1, bf16[2,2,2,256,256]{4,3,2,1,0:T(8,128)(2,1)} %refs_2_.1, bf16[2,2,2,256,256]{4,3,2,1,0:T(8,128)(2,1)} %refs_3_.1, ...), custom_call_target="tpu_custom_call" | custom-call | tf_op jit(solution)/shard_map/pallas_call | solution.py:470
  39.2 1.4 %shard_map.104 = (bf16[2,2,2,256,256]{4,3,2,1,0:T(8,128)(2,1)}, bf16[2,2,2,256,256]{4,3,2,1,0:T(8,128)(2,1)}, f32[2,32,256]{2,1,0:T(8,128)}) custom-call(bf16[2,2,2,256,256]{4,3,2,1,0:T(8,128)(2,1)S(1)} %get-tuple-element.6.local, bf16[3,2,2,2,256,256]{5,4,3,2,1,0:T(8,128)(2,1)S(1)} %get-tuple-element.7.edge, f32[2,32,256]{2,1,0:T(8,128)S(1)} %get-tuple-element.8.grad), custom_call_target="tpu_custom_call" | custom-call | tf_op jit(solution)/shard_map/pallas_call | solution.py:523

commit v6 on v4

--- a/solution.py
+++ b/solution.py
@@ -319,8 +319,14 @@
             out = ((gsum[k, :, cols] + g) * scale).astype(BF16)
             for p in range(groups):
                 gsend[k, p, :, cols] = out[p * rows : (p + 1) * rows]
-        for i in range(groups - 1):
+        for i in same_y:
             share(k, i).start()
+
+        @pl.when(jnp.logical_not(holds))
+        def _():
+            for i in cross_y:
+                share(k, i).start()
+
         for c in range(2):
             x, y = final_x[c], inner[k, f, c]
             t = refl[k] * (x - y)
@@ -338,6 +344,10 @@
         return lax.rem(p + o, groups)
 
     peers = [over(mate, 4), over(mate, 2), over(mate, 6), over(s, 4), mate, over(s, 2), over(s, 6)]
+
+    cross_y = (0, 1, 2, 4)
+    same_y = (3, 5, 6)
+    holds = d < 2
 
     def share(k, i):
         return pltpu.make_async_remote_copy(
@@ -402,6 +412,21 @@
 
     lax.fori_loop(0, 2, final, 0)
 
+    @pl.when(holds)
+    def _():
+        for k in range(2):
+            for i in same_y:
+                share(k, i).wait_recv()
+        for k in range(2):
+            for i in cross_y:
+                share(k, i).start()
+
+    @pl.when(jnp.logical_not(holds))
+    def _():
+        for k in range(2):
+            for i in same_y:
+                share(k, i).wait_recv()
+
     for h in range(HOPS):
         for k in range(2):
             for f in range(2):
@@ -411,9 +436,10 @@
                     link(edge.at[0, k, f], h, k, f).wait_send()
 
     for k in (early, late):
+        for i in cross_y:
+            share(k, i).wait_recv()
         total = gsend[k, s].astype(F32)
         for i in range(groups - 1):
-            share(k, i).wait_recv()
             total = total + grecv[k, i].astype(F32)
         grad_out[k] = total
     for k in range(2):

time: 41 us -> 40.5 us (0.988)
  Pallas kernels: 39.7 us -> 39.2 us
    pallas_call x1, Pallas kernels: 38.3 us -> 37.8 us  [per_device(): pl.pallas_call(lambda *refs: kernel(groups, slabs, *refs), out_shape=(plt...]
where the time goes in v6:
time: 40.5 us; the launch traced here: 39.8 us
  Pallas kernels  39.2 us (97%)
  between operations  0.64 us (2%)
    pallas_call x1, Pallas kernels, per_device(): pl.pallas_call(lambda *refs: kernel(groups, slabs, *refs), out_shape=(plt...  37.8 us
    pallas_call x1, Pallas kernels, per_device(): pl.pallas_call(store, out_shape=[pltpu.HBM(down_state.shape, BF16), pltpu...  1.37 us

profile of v6, /device:TPU:24, one launch (start us, length us, event | category | flops | bytes accessed | tf_op | source)
XLA Modules:
  0.0 39.8 jit_solution(4686989510989285185)
XLA Ops:
  0.6 37.8 %shard_map.103 = (bf16[2,2,2,256,256]{4,3,2,1,0:T(8,128)(2,1)S(1)}, bf16[3,2,2,2,256,256]{5,4,3,2,1,0:T(8,128)(2,1)S(1)}, f32[2,32,256]{2,1,0:T(8,128)S(1)}) custom-call(f32[16]{0:T(128)} %refs_0_.1, s32[2]{0:T(128)} %refs_1_.1, bf16[2,2,2,256,256]{4,3,2,1,0:T(8,128)(2,1)} %refs_2_.1, bf16[2,2,2,256,256]{4,3,2,1,0:T(8,128)(2,1)} %refs_3_.1, ...), custom_call_target="tpu_custom_call" | custom-call | tf_op jit(solution)/shard_map/pallas_call | solution.py:476
  38.5 1.4 %shard_map.104 = (bf16[2,2,2,256,256]{4,3,2,1,0:T(8,128)(2,1)}, bf16[2,2,2,256,256]{4,3,2,1,0:T(8,128)(2,1)}, f32[2,32,256]{2,1,0:T(8,128)}) custom-call(bf16[2,2,2,256,256]{4,3,2,1,0:T(8,128)(2,1)S(1)} %get-tuple-element.6.local, bf16[3,2,2,2,256,256]{5,4,3,2,1,0:T(8,128)(2,1)S(1)} %get-tuple-element.7.edge, f32[2,32,256]{2,1,0:T(8,128)S(1)} %get-tuple-element.8.grad), custom_call_target="tpu_custom_call" | custom-call | tf_op jit(solution)/shard_map/pallas_call | solution.py:529

commit v7 on v6

--- a/solution.py
+++ b/solution.py
@@ -319,14 +319,14 @@
             out = ((gsum[k, :, cols] + g) * scale).astype(BF16)
             for p in range(groups):
                 gsend[k, p, :, cols] = out[p * rows : (p + 1) * rows]
+
+        @pl.when(jnp.logical_not(holds))
+        def _():
+            for i in cross_y:
+                share(k, i).start()
+
         for i in same_y:
             share(k, i).start()
-
-        @pl.when(jnp.logical_not(holds))
-        def _():
-            for i in cross_y:
-                share(k, i).start()
-
         for c in range(2):
             x, y = final_x[c], inner[k, f, c]
             t = refl[k] * (x - y)

time: 40.5 us -> 40.2 us (level)
  no operation moved by 1% of the time
where the time goes in v7:
time: 40.2 us; the launch traced here: 39.5 us
  Pallas kernels  38.8 us (97%)
  between operations  0.64 us (2%)
    pallas_call x1, Pallas kernels, per_device(): pl.pallas_call(lambda *refs: kernel(groups, slabs, *refs), out_shape=(plt...  37.5 us
    pallas_call x1, Pallas kernels, per_device(): pl.pallas_call(store, out_shape=[pltpu.HBM(down_state.shape, BF16), pltpu...  1.37 us

profile of v7, /device:TPU:24, one launch (start us, length us, event | category | flops | bytes accessed | tf_op | source)
XLA Modules:
  0.0 39.5 jit_solution(13915659151007447372)
XLA Ops:
  0.6 37.5 %shard_map.103 = (bf16[2,2,2,256,256]{4,3,2,1,0:T(8,128)(2,1)S(1)}, bf16[3,2,2,2,256,256]{5,4,3,2,1,0:T(8,128)(2,1)S(1)}, f32[2,32,256]{2,1,0:T(8,128)S(1)}) custom-call(f32[16]{0:T(128)} %refs_0_.1, s32[2]{0:T(128)} %refs_1_.1, bf16[2,2,2,256,256]{4,3,2,1,0:T(8,128)(2,1)} %refs_2_.1, bf16[2,2,2,256,256]{4,3,2,1,0:T(8,128)(2,1)} %refs_3_.1, ...), custom_call_target="tpu_custom_call" | custom-call | tf_op jit(solution)/shard_map/pallas_call | solution.py:476
  38.1 1.4 %shard_map.104 = (bf16[2,2,2,256,256]{4,3,2,1,0:T(8,128)(2,1)}, bf16[2,2,2,256,256]{4,3,2,1,0:T(8,128)(2,1)}, f32[2,32,256]{2,1,0:T(8,128)}) custom-call(bf16[2,2,2,256,256]{4,3,2,1,0:T(8,128)(2,1)S(1)} %get-tuple-element.6.local, bf16[3,2,2,2,256,256]{5,4,3,2,1,0:T(8,128)(2,1)S(1)} %get-tuple-element.7.edge, f32[2,32,256]{2,1,0:T(8,128)S(1)} %get-tuple-element.8.grad), custom_call_target="tpu_custom_call" | custom-call | tf_op jit(solution)/shard_map/pallas_call | solution.py:529
